TPU v7x, 512 devices: a whole 4x8x8 slice. The times are simulated.
512 devices in a mesh: sens: 32 (over y, x), tm: 16 (over z, core).
Axes of the slice: x: 4, y: 8, z: 8, core: 2. Of those that a mesh axis runs over, the one named last changes fastest.
Arguments:
- observed: float32 [64, 16384], P('tm', 'sens'), may hold values from -16 to 16
- loadings: bfloat16 [16384, 512], P('sens'), may hold values from -0.046875 to 0.046875
- noise_prec: float32 [16384], P('sens'), may hold values from 0.02 to 0.2
- dynamics: float32 [512, 512], replicated, as said below
- prior_prec: float32 [512, 512], replicated, as said below
Outputs:
- filtered: float32 [64, 512], P('tm')
- smoothed: float32 [64, 512], P('tm')
Inputs may be any that keep to these rules, and one draw needn't show every extreme that they name: `dynamics`: a real square transition matrix. `prior_prec`: symmetric positive definite; commutes with dynamics.
All inputs are finite; a program needn't handle non-finite values.
Results may differ from a plain program's by a relative error of at most 0.0003.
Values sent between devices are 32-bit elements; how exact they have to be, the bound alone decides.
No kernel may reach another device: no remote copies, remote signals or barrier semaphores. Data moves between devices by JAX's collectives and lax.ppermute only.
A program may use at most 64 MiB of HBM per device.

v0:
```python
import jax
import jax.numpy as jnp
from jax import lax
from jax.sharding import PartitionSpec as P

precise = lax.Precision.HIGHEST


def in_blocks(shard, dim, peers):
    before, after = (shard.shape[:dim], shard.shape[dim + 1 :])
    return jnp.moveaxis(shard.reshape(*before, peers, -1, *after), dim, 0)


def summed_on_arrival(shard, axis, dim):
    pieces = in_blocks(shard, dim, lax.axis_size(axis))
    arrived = lax.all_to_all(pieces, axis, split_axis=0, concat_axis=0, tiled=True)
    return arrived.sum(axis=0)


def filled_up(lines, peers):
    spare = -lines.shape[0] % peers
    if not spare:
        return lines
    return jnp.concatenate([lines, jnp.zeros((spare, *lines.shape[1:]), lines.dtype)])


def joined_along(pieces, dim):
    shape = list(pieces.shape[1:])
    shape[dim] *= pieces.shape[0]
    return jnp.moveaxis(pieces, 0, dim).reshape(shape)


def sent_to_all(shard, axis):
    copies = jnp.broadcast_to(shard, (lax.axis_size(axis), *shard.shape))
    return lax.all_to_all(copies, axis, split_axis=0, concat_axis=0, tiled=True)


def gather_directly(shard, axis, dim):
    return joined_along(sent_to_all(shard, axis), dim)


def nested_sum(shard, axes):
    own = summed_on_arrival(filled_up(shard, lax.axis_size(axes)), axes, 0)
    whole = gather_directly(own, axes, 0)
    return whole[: len(shard)].reshape(shard.shape)


def packed_total(arrays, axis):
    line, at, gathered = (jnp.concatenate([a.reshape(-1) for a in arrays]), 0, [])
    subtotal = nested_sum(line, axis)
    for a in arrays:
        gathered.append(subtotal[at : at + a.size].reshape(a.shape))
        at += a.size
    return tuple(gathered)


def inverse_spd(matrix):
    lower_factor = jnp.linalg.cholesky(matrix)
    identity = jnp.eye(matrix.shape[0], dtype=matrix.dtype)
    lower_inv = lax.linalg.triangular_solve(lower_factor, identity, left_side=True, lower=True)
    return jnp.dot(lower_inv.T, lower_inv, precision=precise)


def model_mats(gram_mat, prior_prec, dynamics):
    post_cov = inverse_spd(gram_mat + prior_prec)
    forward = jnp.dot(post_cov, jnp.dot(prior_prec, dynamics, precision=precise), precision=precise)
    gain_mat = jnp.dot(
        post_cov, jnp.dot(dynamics.T, prior_prec, precision=precise), precision=precise
    )
    identity = jnp.eye(gram_mat.shape[0], dtype=gram_mat.dtype)
    keep_mat = identity - jnp.dot(gain_mat, dynamics, precision=precise)
    return (post_cov, forward, gain_mat, keep_mat)


def matrix_power(matrix, times_count):
    result = None
    square = matrix
    for bit_pos in range(times_count.bit_length()):
        if bit_pos > 0:
            square = jnp.dot(square, square, precision=precise)
        if times_count >> bit_pos & 1:
            result = square
    return result


def row_gram(rows, weights):
    return lax.dot_general(
        rows * weights[:, None],
        rows,
        (((0,), (0,)), ((), ())),
        precision=precise,
        preferred_element_type=jnp.float32,
    )


def shards(observed, loadings, noise_prec, dynamics, prior_prec):
    load_rows = loadings.astype(jnp.float32)
    state_dim = load_rows.shape[1]
    step_count = observed.shape[0]
    info_part = jnp.dot(observed * noise_prec[None, :], load_rows, precision=precise)
    gram_part = row_gram(load_rows, noise_prec)
    gram_mat, info_rows = packed_total((gram_part, info_part), "sens")
    post_cov, forward, gain_mat, keep_mat = model_mats(gram_mat, prior_prec, dynamics)
    drive_rows = lax.dot_general(
        info_rows,
        post_cov,
        (((1,), (1,)), ((), ())),
        precision=precise,
        preferred_element_type=jnp.float32,
    )
    forward_pow = matrix_power(forward, step_count)
    gain_pow = matrix_power(gain_mat, step_count)
    blocks = lax.axis_size("tm")
    my_block = lax.axis_index("tm")
    is_top = my_block == blocks - 1
    zero_vec = jnp.zeros((state_dim,), jnp.float32)
    local_state = zero_vec
    local_rows = []
    for time_step in range(step_count):
        local_state = jnp.dot(forward, local_state, precision=precise) + drive_rows[time_step]
        local_rows.append(local_state)
    block_ends = lax.all_gather(local_state[None, :], "tm", axis=0, tiled=True)

    def forward_turn(block_index, carried):
        return jnp.where(
            block_index < my_block,
            jnp.dot(forward_pow, carried, precision=precise) + block_ends[block_index],
            carried,
        )

    entering = lax.fori_loop(0, blocks, forward_turn, zero_vec)
    correction = entering
    filt_rows = []
    for time_step in range(step_count):
        correction = jnp.dot(forward, correction, precision=precise)
        filt_rows.append(local_rows[time_step] + correction)
    filtered = jnp.stack(filt_rows)
    kept_part = lax.dot_general(
        filtered,
        keep_mat,
        (((1,), (1,)), ((), ())),
        precision=precise,
        preferred_element_type=jnp.float32,
    )
    top_tail = jnp.where(is_top, jnp.dot(dynamics, filt_rows[-1], precision=precise), zero_vec)
    back_state = top_tail
    back_rows = [None] * step_count
    for time_step in range(step_count - 1, -1, -1):
        back_state = kept_part[time_step] + jnp.dot(gain_mat, back_state, precision=precise)
        back_rows[time_step] = back_state
    block_starts = lax.all_gather(back_state[None, :], "tm", axis=0, tiled=True)

    def backward_turn(turn_number, carried):
        block_index = blocks - 1 - turn_number
        return jnp.where(
            block_index > my_block,
            jnp.dot(gain_pow, carried, precision=precise) + block_starts[block_index],
            carried,
        )

    leaving = lax.fori_loop(0, blocks, backward_turn, zero_vec)
    correction = leaving
    smooth_rows = [None] * step_count
    for time_step in range(step_count - 1, -1, -1):
        correction = jnp.dot(gain_mat, correction, precision=precise)
        smooth_rows[time_step] = back_rows[time_step] + correction
    return (filtered, jnp.stack(smooth_rows))


def solution(mesh):
    placed = (P("tm", "sens"), P("sens", None), P("sens"), P(), P())
    return jax.shard_map(
        shards,
        mesh=mesh,
        in_specs=placed,
        out_specs=(P("tm", None), P("tm", None)),
        check_vma=False,
    )
```

profile of v0, /device:TPU:1, one launch (start us, length us, event | category | flops | bytes accessed | tf_op | source)
XLA Modules:
  0.0 376.7 jit_solution(5441655782103358515)
XLA Ops:
  0.7 2.4 convolution_bitcast_fusion
  4.8 2.5 all_to_all.10
  7.4 40.0 %all_to_all.15 = f32[32,1,8256]{2,1,0:T(1,128)} all-to-all(f32[32,1,8256]{2,1,0:T(1,128)S(1)} %all_to_all.10), channel_id=1, replica_groups=mesh['sens'=32,'tm'=16] {'sens'}, dimensions={0} | all-to-all | bytes 2113536 | tf_op jit(solution)/shard_map/all_to_all | solution.py:16
  50.8 4.3 %all-to-all-start.1 = ((f32[32,1,8256]{2,1,0:T(1,128)}), f32[32,1,8256]{2,1,0:T(1,128)S(1)}, u32[]{:S(2)}, u32[]{:S(2)}) async-start(f32[32,1,8256]{2,1,0:T(1,128)} %broadcast_in_dim.16), calls=%async_computation.1 | async-start | bytes 2129920 | tf_op jit(solution)/shard_map/all_to_all | solution.py:35
  58.3 2.9 fusion.67
  61.2 2.9 fusion.75
  64.1 16.7 %all-to-all-done.1 = f32[32,1,8256]{2,1,0:T(1,128)S(1)} async-done(((f32[32,1,8256]{2,1,0:T(1,128)}), f32[32,1,8256]{2,1,0:T(1,128)S(1)}, u32[]{:S(2)}, u32[]{:S(2)}) %all-to-all-start.1) | async-done | bytes 1056800 | tf_op jit(solution)/shard_map/all_to_all | solution.py:35
  80.7 3.8 %reduce.25 = f32[32,8256]{1,0:T(8,128)} reduce(f32[32,1,8256]{2,1,0:T(1,128)S(1)} %all-to-all-done.1, f32[]{:T(128)} %constant.233), dimensions={1}, to_apply=%all_to_all.12.reduce_sub_computation | reduce | bytes 2113540 | tf_op jit(solution)/shard_map/all_to_all | solution.py:35
  93.3 12.1 %cholesky.104 = f32[128,128]{1,0:T(8,128)S(1)} custom-call(f32[128,128]{1,0:T(8,128)S(1)} %cholesky.266), custom_call_target="Cholesky" | custom-call | tf_op jit(solution)/shard_map/jit(cholesky)/cholesky | solution.py:58
  105.5 9.8 %custom-call.30 = f32[1,128,128]{1,2,0:T(8,128)S(1)} custom-call(f32[1,128,128]{2,1,0:T(8,128)S(1)} %get-tuple-element.313), custom_call_target="InvertDiagBlocksLowerTriangular" | custom-call | tf_op jit(solution)/shard_map/jit(cholesky)/cholesky | solution.py:58
  117.9 11.7 %cholesky.217 = f32[128,128]{1,0:T(8,128)S(1)} custom-call(f32[128,128]{1,0:T(8,128)S(1)} %cholesky.270), custom_call_target="Cholesky" | custom-call | tf_op jit(solution)/shard_map/jit(cholesky)/cholesky | solution.py:58
  129.6 9.8 %custom-call.31 = f32[1,128,128]{1,2,0:T(8,128)S(1)} custom-call(f32[1,128,128]{2,1,0:T(8,128)S(1)} %get-tuple-element.310), custom_call_target="InvertDiagBlocksLowerTriangular" | custom-call | tf_op jit(solution)/shard_map/jit(cholesky)/cholesky | solution.py:58
  141.0 11.9 %cholesky.238 = f32[128,128]{1,0:T(8,128)S(1)} custom-call(f32[128,128]{1,0:T(8,128)S(1)} %cholesky.275), custom_call_target="Cholesky" | custom-call | tf_op jit(solution)/shard_map/jit(cholesky)/cholesky | solution.py:58
  152.9 9.8 %custom-call.32 = f32[1,128,128]{1,2,0:T(8,128)S(1)} custom-call(f32[1,128,128]{2,1,0:T(8,128)S(1)} %get-tuple-element.307), custom_call_target="InvertDiagBlocksLowerTriangular" | custom-call | tf_op jit(solution)/shard_map/jit(cholesky)/cholesky | solution.py:58
  164.2 11.7 %cholesky.255 = f32[128,128]{1,0:T(8,128)S(1)} custom-call(f32[128,128]{1,0:T(8,128)S(1)} %convolution_subtract_fusion.6), custom_call_target="Cholesky" | custom-call | tf_op jit(solution)/shard_map/jit(cholesky)/cholesky | solution.py:58
  181.6 14.5 %while.31 = (s32[]{:T(128)}, f32[512,512]{1,0:T(8,128)}, s32[4,2]{0,1:T(2,128)S(1)}, f32[4,128,128]{2,1,0:T(8,128)}, s32[]{:T(128)}) while((s32[]{:T(128)}, f32[512,512]{1,0:T(8,128)}, s32[4,2]{0,1:T(2,128)S(1)}, f32[4,128,128]{2,1,0:T(8,128)}, s32[]{:T(128)}) %tuple.99), condition=%wide.while_cond, body=%wide.while_body.sunk | while | flops 2 | bytes 132205 | solution.py:60
  182.3 3.0 bitcast_dynamic-update-slice_fusion.2
  185.9 3.0 bitcast_dynamic-update-slice_fusion.2
  189.6 3.0 bitcast_dynamic-update-slice_fusion.2
  193.2 2.9 bitcast_dynamic-update-slice_fusion.2
  196.1 40.5 %custom-call.33 = f32[4,128,128]{1,2,0:T(8,128)S(1)} custom-call(f32[4,128,128]{2,1,0:T(8,128)} %get-tuple-element.237), custom_call_target="InvertDiagBlocksLowerTriangular" | custom-call | tf_op jit(solution)/shard_map/triangular_solve | solution.py:60
  243.5 1.9 fusion
  249.5 1.9 fusion.69
  251.3 1.9 fusion.76
  253.2 3.0 convolution_subtract_fusion
  256.2 2.9 fusion.83
  262.1 2.8 fusion.70
  265.0 26.9 %all-gather.2 = f32[16,1,512]{2,1,0:T(1,128)S(1)} all-gather(f32[1,1,512]{2,1,0:T(1,128)S(1)} %bitcast.230), channel_id=2, replica_groups=mesh['sens'=32,'tm'=16] {'tm'}, dimensions={0}, use_global_device_ids=true | all-gather | bytes 34816 | tf_op jit(solution)/shard_map/all_gather | solution.py:122
  291.9 36.4 %while.32 = (s32[]{:T(128)}, f32[512]{0:T(512)S(1)}, s32[]{:T(128)}, f32[512,512]{1,0:T(8,128)}, f32[16,512]{1,0:T(8,128)S(1)}, /*index=5*/s32[]{:T(128)}, s32[]{:T(128)}) while((s32[]{:T(128)}, f32[512]{0:T(512)S(1)}, s32[]{:T(128)}, f32[512,512]{1,0:T(8,128)}, f32[16,512]{1,0:T(8,128)S(1)}, /*index=5*/s32[]{:T(128)}, ...), condition=%wide.region_10.11_spmd.clone, body=%wide.region_9.10_spmd.clone.sunk | while | flops 3147780 | bytes 1069166 | solution.py:131
  291.9 2.2 fusion.155
  294.1 2.2 fusion.155
  296.4 2.2 fusion.155
  298.7 2.2 fusion.155
  301.0 2.2 fusion.155
  303.2 2.2 fusion.155
  305.5 2.2 fusion.155
  307.8 2.2 fusion.155
  310.1 2.2 fusion.155
  312.3 2.2 fusion.155
  314.6 2.2 fusion.155
  316.9 2.2 fusion.155
  319.2 2.2 fusion.155
  321.4 2.2 fusion.155
  323.7 2.2 fusion.155
  326.0 2.2 fusion.155
  335.3 1.9 fusion.84
  340.2 14.5 %all-gather.3 = f32[16,1,512]{2,1,0:T(1,128)S(1)} all-gather(f32[1,1,512]{2,1,0:T(1,128)S(1)} %bitcast.229), channel_id=3, replica_groups=mesh['sens'=32,'tm'=16] {'tm'}, dimensions={0}, use_global_device_ids=true | all-gather | bytes 34816 | tf_op jit(solution)/shard_map/all_gather | solution.py:151
  354.7 17.1 %while.33 = (s32[]{:T(128)}, f32[512]{0:T(512)S(1)}, s32[]{:T(128)}, f32[512,512]{1,0:T(8,128)S(1)}, f32[16,512]{1,0:T(8,128)S(1)}, /*index=5*/s32[]{:T(128)}, s32[]{:T(128)}, s32[]{:T(128)}, s32[]{:T(128)}) while((s32[]{:T(128)}, f32[512]{0:T(512)S(1)}, s32[]{:T(128)}, f32[512,512]{1,0:T(8,128)S(1)}, f32[16,512]{1,0:T(8,128)S(1)}, ...), condition=%wide.region_12.13_spmd.clone, body=%wide.region_11.12_spmd.clone.sunk | while | flops 3147784 | bytes 1069228 | solution.py:161
  (230 shorter events, 73.9 us)
Async XLA Ops:
  0.6 57.7 %copy-start = (f32[512,512]{1,0:T(8,128)S(1)}, f32[512,512]{1,0:T(8,128)}, u32[]{:S(2)}) copy-start(f32[512,512]{1,0:T(8,128)} %param.12) | copy-start | bytes 3145732
  0.6 2.5 copy-start.3
  0.7 2.5 copy-start.10
  0.7 2.5 copy-start.9
  50.8 4.3 %copy-start.1 = (f32[512,512]{1,0:T(8,128)S(1)}, f32[512,512]{1,0:T(8,128)}, u32[]{:S(2)}) copy-start(f32[512,512]{1,0:T(8,128)} %param.13) | copy-start | bytes 3145732
  50.8 29.9 %all-to-all-start.1 = ((f32[32,1,8256]{2,1,0:T(1,128)}), f32[32,1,8256]{2,1,0:T(1,128)S(1)}, u32[]{:S(2)}, u32[]{:S(2)}) async-start(f32[32,1,8256]{2,1,0:T(1,128)} %broadcast_in_dim.16), calls=%async_computation.1 | async-start | bytes 2129920 | tf_op jit(solution)/shard_map/all_to_all | solution.py:35
  92.3 1.0 copy-start.7
  245.4 1.2 copy-start.5
  249.5 1.9 copy-start.4
  330.2 2.1 copy-start.6
  332.3 2.0 copy-start.8
  333.3 2.0 copy-start.2
where the time goes:
time: 382 us; the launch traced here: 377 us
  other arithmetic  134 us (35%)
  matrix products  108 us (28%)
  blocking collectives  81.5 us (21%)
  local copies, waits for them, and re-layouts  26.8 us (7%)
  waiting for transfers between devices  16.7 us (4%)
  starting transfers between devices  4.27 us (1%)
  between operations  3.87 us (1%)
    another operation x14, other arithmetic, inverse_spd(): lower_factor = jnp.linalg.cholesky(matrix)  79 us
    another operation x3, other arithmetic, inverse_spd(): lax.linalg.triangular_solve(lower_factor, identity, left_side=True, lower...  41.6 us
    all_to_all x1, blocking collectives, summed_on_arrival(): lax.all_to_all(pieces, axis, split_axis=0, concat_axis=0, tiled=True)  40 us
    dot_general x16, matrix products, forward_turn(): jnp.dot(forward_pow, carried, precision=precise) + block_ends[block_index]  35.2 us
    all_gather x1, blocking collectives, shards(): block_ends = lax.all_gather(local_state[None, :], 'tm', axis=0, tiled=True)  26.9 us
    all_to_all x1, waiting for transfers between devices, sent_to_all(): return lax.all_to_all(copies, axis, split_axis=0, concat_axis=0, tiled=True)  16.7 us
    dot_general x16, matrix products, backward_turn(): jnp.dot(gain_pow, carried, precision=precise) + block_starts[block_index]  15.7 us
    all_gather x1, blocking collectives, shards(): block_starts = lax.all_gather(back_state[None, :], 'tm', axis=0, tiled=True)  14.5 us
  transfers between devices with their start and end apart: 1, of which 1 were waited for; matrix products, arithmetic and copies ran while one was open for 2% of the time, Pallas kernels for 0%

commit v1 on v0

v1 whole, which is shorter than its diff:
```python
from functools import partial

import jax
import jax.numpy as jnp
from jax import lax
from jax.experimental import pallas as pl
from jax.experimental.pallas import tpu as pltpu
from jax.sharding import PartitionSpec as P

f32 = jnp.float32
bf16 = jnp.bfloat16
R = 512


def dot1(a, b, ca=1, cb=0):
    return lax.dot_general(a, b, (((ca,), (cb,)), ((), ())), preferred_element_type=f32)


def split(a):
    hi = a.astype(bf16)
    return hi, (a - hi.astype(f32)).astype(bf16)


def dot3(a, b, ca=1, cb=0):
    return dot1(a[0], b[0], ca, cb) + (dot1(a[0], b[1], ca, cb) + dot1(a[1], b[0], ca, cb))


def dot6(a, b, ca=1, cb=0):
    return lax.dot_general(
        a, b, (((ca,), (cb,)), ((), ())), precision=lax.Precision.HIGHEST, preferred_element_type=f32
    )


def eye():
    return (lax.broadcasted_iota(jnp.int32, (R, R), 0) == lax.broadcasted_iota(jnp.int32, (R, R), 1)).astype(f32)


def sum_sq(x):
    return jnp.sum(x * x)


def sweep_inverse(ref):
    lane = lax.broadcasted_iota(jnp.int32, (1, R), 1)
    row_at = lax.broadcasted_iota(jnp.int32, (R, 1), 0)

    def body(k, _):
        a = ref[...]
        row = ref[pl.ds(k, 1), :]
        here = lane == k
        pivot = jnp.sum(jnp.where(here, row, 0.0), axis=1, keepdims=True)
        col = jnp.sum(jnp.where(here, a, 0.0), axis=1, keepdims=True)
        col = jnp.where(row_at == k, 0.0, col)
        row = jnp.where(here, 1.0, row) / pivot
        ref[...] = jnp.where(here, 0.0, a) - col * row
        ref[pl.ds(k, 1), :] = row
        return 0

    lax.fori_loop(0, R, body, 0)


ROWS = 24
INFO = 640


def partials(tm_ref, obs_ref, load_ref, noise_ref, out_ref):
    noise = noise_ref[...]
    column = jnp.broadcast_to(noise, (128, R)).T

    def weighted(i):
        return split(load_ref[:, 128 * i : 128 * i + 128].astype(f32) * column)

    def pairs(i, lo, at):
        rows = load_ref[:, lo:]
        hi, rest = weighted(i)
        blocks = dot1(hi, rows, 0, 0) + dot1(rest, rows, 0, 0)
        for n in range((R - lo) // 128):
            out_ref[at + 128 * n : at + 128 * n + 128, :] = blocks[:, 128 * n : 128 * n + 128]

    def one(i, at):
        rows = load_ref[:, 128 * i : 128 * i + 128]
        hi, rest = weighted(i)
        out_ref[at : at + 128, :] = dot1(hi, rows, 0, 0) + dot1(rest, rows, 0, 0)

    first = lax.rem(tm_ref[0], 2) == 0

    @pl.when(first)
    def _():
        pairs(0, 0, 0)
        one(1, 512)

    @pl.when(jnp.logical_not(first))
    def _():
        pairs(1, 256, 0)
        pairs(2, 256, 256)
        one(3, 512)

    hi, rest = split(obs_ref[...] * noise)
    rows = load_ref[...]
    info = dot1(hi, rows) + dot1(rest, rows)
    for t in range(4):
        for c in range(4):
            out_ref[INFO + 4 * t + c : INFO + 4 * t + c + 1, :] = info[t : t + 1, 128 * c : 128 * c + 128]
    out_ref[INFO + 16 :, :] = jnp.zeros((32 * ROWS - INFO - 16, 128), f32)


def sum_and_spread(in_ref, out_ref):
    total = in_ref[0]
    for n in range(1, 32):
        total = total + in_ref[n]
    for n in range(32):
        out_ref[n] = total


def prep_a(dyn_ref, prior_ref, wt_ref, nn_ref, x_ref):
    prior = prior_ref[...]
    psplit = split(prior)
    wt = dot6(dyn_ref[...], prior, 0, 0)
    wt_ref[...] = wt
    nn_ref[...] = dot6(wt, dyn_ref[...])
    col = jnp.sum(jnp.abs(prior), axis=0, keepdims=True)
    start = 1.0 / jnp.max(col, axis=1, keepdims=True)
    ident = eye()
    x = ident * start
    ph = psplit[0]
    x = start * (2.0 * ident - start * prior)
    x_ref[...] = x

    def body(k, _):
        x = x_ref[...]
        xh = x.astype(bf16)
        t = dot1(ph, xh)
        x_ref[...] = 2.0 * x - dot1(xh, t.astype(bf16))
        return 0

    lax.fori_loop(0, 6, body, 0)


def refine(times_mat, x_ref, r_ref, done2, cap):
    ident = eye()

    def residual():
        r = ident - times_mat(x_ref[...])
        r_ref[...] = r
        return sum_sq(r)

    def cond(c):
        k, n2, old = c
        return (n2 > done2) & (k < cap) & (n2 < 0.98 * old)

    def body(c):
        k, n2, _ = c
        x = x_ref[...]
        x_ref[...] = x + dot3(split(x), split(r_ref[...]))
        return k + 1, residual(), n2

    n0 = residual()
    return lax.while_loop(cond, body, (jnp.int32(0), n0, jnp.float32(jnp.inf)))


def prep_b(prior_ref, x_in, x_ref, r_ref):
    x_ref[...] = x_in[...]
    _, n2, _ = refine(lambda v: dot3(split(prior_ref[...]), split(v)), x_ref, r_ref, 1e-5, 40)

    @pl.when(jnp.logical_not(n2 < 0.05))
    def _():
        x_ref[...] = prior_ref[...]
        sweep_inverse(x_ref)


PAIRS = ((0, 0), (0, 1), (0, 2), (0, 3), (1, 1), (1, 2), (1, 3), (2, 2), (2, 3), (3, 3))


def invert(tm_ref, own_ref, other_ref, prior_ref, pinv_ref, wt_ref, a_ref, x_ref, ft_ref, g_ref, r_ref):
    first = lax.rem(tm_ref[0], 2) == 0
    for n, (i, j) in enumerate(PAIRS):
        at = (n % 5) * 128
        mine, theirs = own_ref[at : at + 128, :], other_ref[at : at + 128, :]
        blk = jnp.where(first, mine, theirs) if n < 5 else jnp.where(first, theirs, mine)
        g_ref[128 * i : 128 * i + 128, 128 * j : 128 * j + 128] = blk
        if i != j:
            g_ref[128 * j : 128 * j + 128, 128 * i : 128 * i + 128] = blk.T
    gram = g_ref[...]
    a = prior_ref[...] + gram
    a_ref[...] = a
    pinv = pinv_ref[...]
    ph = pinv.astype(bf16)
    e = dot1(gram.astype(bf16), ph)
    size = jnp.sqrt(sum_sq(e))
    theta = jnp.where(size < 0.9, 1.0, 2.0 / (2.0 + size))
    r0 = (1.0 - theta) * eye() - theta * e
    rh = r0.astype(bf16)
    t = dot1(rh, rh)
    s = r0 + t + dot1(rh, t.astype(bf16))
    x_ref[...] = theta * (pinv + dot1(ph, s.astype(bf16)))
    _, n2, _ = refine(lambda v: dot6(a_ref[...], v), x_ref, r_ref, 1e-4, 60)

    good = n2 < 1e-4

    @pl.when(good)
    def _():
        x = x_ref[...]
        r = r_ref[...]
        rh = r.astype(bf16)
        x_ref[...] = x + dot1(x.astype(bf16), (r + dot1(rh, rh)).astype(bf16))

    @pl.when(jnp.logical_not(good))
    def _():
        x_ref[...] = a_ref[...]
        sweep_inverse(x_ref)

    ft_ref[...] = dot6(wt_ref[...], x_ref[...])


def scans(tm_ref, info_ref, x_ref, ft_ref, a_ref, nn_ref, filt_ref, smooth_ref, f_ref, s_ref):
    T = 64
    x = split(x_ref[...])
    parts = [info_ref[pl.ds(c, T, stride=4), :] for c in range(4)]
    info = jnp.concatenate(parts, axis=1)
    y = dot3(split(info), x)
    f = ft_ref[...]
    powers = [split(f)]
    ident = eye()
    c = jnp.sum(jnp.sum(f * ident, axis=0, keepdims=True), axis=1, keepdims=True) * (1.0 / R)
    e = f - c * ident
    es = split(e)
    f = c * (f + e) + dot3(es, es)
    powers.append(split(f))
    for _ in range(4):
        f = dot3(powers[-1], powers[-1])
        powers.append(split(f))
    step = lax.broadcasted_iota(jnp.int32, (T, 1), 0)

    def later(v, k):
        return jnp.where(step >= k, pltpu.roll(v, k, 0), 0.0)

    def sooner(v, k):
        return jnp.where(step < T - k, pltpu.roll(v, T - k, 0), 0.0)

    for n, p in enumerate(powers):
        y = y + later(dot3(split(y), p), 1 << n)
    f_ref[...] = y
    nn = nn_ref[...]
    ys = split(y)
    u = dot3(ys, split(a_ref[...] - nn))
    tail = dot3(split(y[T - 8 :, :]), split(nn))
    u = u + jnp.where(step == T - 1, jnp.concatenate([jnp.zeros((T - 8, R), f32), tail], axis=0), 0.0)
    for n, p in enumerate(powers):
        u = u + sooner(dot3(split(u), p, 1, 1), 1 << n)
    s_ref[...] = dot3(split(u), x)
    at = pl.multiple_of(8 * lax.div(tm_ref[0], 2), 8)
    half = lax.rem(tm_ref[0], 2) == 0
    fb = f_ref[pl.ds(at, 8), :]
    sb = s_ref[pl.ds(at, 8), :]
    filt_ref[...] = jnp.where(half, fb[0:4], fb[4:8])
    smooth_ref[...] = jnp.where(half, sb[0:4], sb[4:8])


vm = partial(pltpu.VMEM, (R, R))
mat = jax.ShapeDtypeStruct((R, R), f32)
smem = pl.BlockSpec(memory_space=pltpu.SMEM)
vmem = pl.BlockSpec(memory_space=pltpu.VMEM)


def prep_first(dyn, prior):
    return pl.pallas_call(prep_a, out_shape=(mat, mat, mat), name="prep_a")(dyn, prior)


def prep_second(prior, x):
    return pl.pallas_call(prep_b, out_shape=mat, scratch_shapes=[vm(f32)], name="prep_b")(prior, x)


def inverse(tm, own, other, prior, pinv, wt):
    return pl.pallas_call(
        invert,
        out_shape=(mat, mat, mat),
        in_specs=[smem] + [vmem] * 5,
        scratch_shapes=[vm(f32), vm(f32)],
        name="invert",
    )(tm, own, other, prior, pinv, wt)


def time_scans(tm, info, x, ft, a, nn):
    out = jax.ShapeDtypeStruct((4, R), f32)
    return pl.pallas_call(
        scans,
        out_shape=(out, out),
        in_specs=[smem] + [vmem] * 5,
        scratch_shapes=[pltpu.VMEM((64, R), f32)] * 2,
        name="scans",
    )(tm, info, x, ft, a, nn)


def local_partials(tm, observed, loadings, noise):
    return pl.pallas_call(
        partials,
        out_shape=jax.ShapeDtypeStruct((32 * ROWS, 128), f32),
        in_specs=[smem] + [vmem] * 3,
        name="partials",
    )(tm, observed, loadings, noise)


def summed(pieces):
    return pl.pallas_call(
        sum_and_spread, out_shape=jax.ShapeDtypeStruct(pieces.shape, f32), name="sum_and_spread"
    )(pieces)


def exchange(pieces, axis):
    return lax.all_to_all(pieces, axis, split_axis=0, concat_axis=0, tiled=True)


def shards(observed, loadings, noise_prec, dynamics, prior_prec):
    tm = lax.axis_index("tm").astype(jnp.int32).reshape(1)
    send = local_partials(tm, observed, loadings, noise_prec.reshape(1, R))
    send, dynamics, prior_prec = lax.optimization_barrier((send, dynamics, prior_prec))
    pieces = exchange(send.reshape(32, ROWS, 128), "sens")
    wt, nn, x0 = prep_first(dynamics, prior_prec)
    total = summed(pieces)
    total, x0 = lax.optimization_barrier((total, x0))
    own = exchange(total, "sens").reshape(32 * ROWS, 128)
    pinv = prep_second(prior_prec, x0)
    own, pinv = lax.optimization_barrier((own, pinv))
    other = lax.ppermute(own, "tm", [(i, i ^ 1) for i in range(16)])
    info = jnp.broadcast_to(own[INFO : INFO + 16], (16, 16, 128))
    info = exchange(info, "tm").reshape(256, 128)
    a, x, ft = inverse(tm, own, other, prior_prec, pinv, wt)
    return time_scans(tm, info, x, ft, a, nn)


def solution(mesh):
    return jax.shard_map(
        shards,
        mesh=mesh,
        in_specs=(P("tm", "sens"), P("sens", None), P("sens"), P(), P()),
        out_specs=(P("tm", None), P("tm", None)),
        check_vma=False,
    )
```

time: 382 us -> 91.8 us (0.24); the launches traced: 377 us -> 91.3 us
  other arithmetic: 134 us -> 0 us
  matrix products: 108 us -> 0 us
  blocking collectives: 81.5 us -> 0 us
  Pallas kernels: 0 us -> 45.3 us
  starting transfers between devices: 4.27 us -> 32.4 us
  local copies, waits for them, and re-layouts: 26.8 us -> 2.82 us
  waiting for transfers between devices: 16.7 us -> 10.1 us
    another operation x19 -> x0, other arithmetic: 121 us -> none  [the longest x14 79 us: inverse_spd(): lower_factor = jnp.linalg.cholesky(matrix)]
    dot_general x63 -> x0, matrix products: 96.2 us -> none  [the longest x16 35.2 us: forward_turn(): jnp.dot(forward_pow, carried, precision=precise) + block_ends[block_index]]
    pallas_call x0 -> x6, Pallas kernels: none -> 45.3 us  [the longest x1 13.9 us: time_scans(): pl.pallas_call(scans, out_shape=(out, out), in_specs=[smem] + [vmem] * 5,...]
    all_gather x2 -> x0, blocking collectives: 41.4 us -> none  [the longest x1 26.9 us: shards(): block_ends = lax.all_gather(local_state[None, :], 'tm', axis=0, tiled=True)]
    all_to_all x1 -> x0, blocking collectives: 40 us -> none  [summed_on_arrival(): lax.all_to_all(pieces, axis, split_axis=0, concat_axis=0, tiled=True)]
    all_to_all x1 -> x3, starting transfers between devices: 4.27 us -> 27.3 us  [exchange(): return lax.all_to_all(pieces, axis, split_axis=0, concat_axis=0, tiled=True)]
    another operation x17 -> x0, local copies, waits for them, and re-layouts: 14.6 us -> none
    another operation x13 -> x0, matrix products: 12.3 us -> none  [the longest x7 6.83 us: inverse_spd(): lax.linalg.triangular_solve(lower_factor, identity, left_side=True, lower...]
  transfers between devices with their start and end apart: 1 -> 4, of which waited for: 1 -> 2; matrix products, arithmetic and copies ran while one was open for 2% -> 1% of each run, Pallas kernels for 0% -> 30%
where the time goes in v1:
time: 91.8 us; the launch traced here: 91.3 us
  Pallas kernels  45.3 us (49%)
  starting transfers between devices  32.4 us (35%)
  waiting for transfers between devices  10.1 us (11%)
  local copies, waits for them, and re-layouts  2.82 us (3%)
    all_to_all x3, starting transfers between devices, exchange(): return lax.all_to_all(pieces, axis, split_axis=0, concat_axis=0, tiled=True)  27.3 us
    pallas_call x1, Pallas kernels, time_scans(): pl.pallas_call(scans, out_shape=(out, out), in_specs=[smem] + [vmem] * 5,...  13.9 us
    pallas_call x1, Pallas kernels, prep_first(): pl.pallas_call(prep_a, out_shape=(mat, mat, mat), name='prep_a')(dyn, prior)  11 us
    all_to_all x3, waiting for transfers between devices, exchange(): return lax.all_to_all(pieces, axis, split_axis=0, concat_axis=0, tiled=True)  10.1 us
    pallas_call x1, Pallas kernels, inverse(): pl.pallas_call(invert, out_shape=(mat, mat, mat), in_specs=[smem] + [vmem...  10 us
    pallas_call x1, Pallas kernels, prep_second(): pl.pallas_call(prep_b, out_shape=mat, scratch_shapes=[vm(f32)], name='pre...  5.94 us
    ppermute x1, starting transfers between devices, shards(): other = lax.ppermute(own, 'tm', [(i, i ^ 1) for i in range(16)])  5.09 us
    pallas_call x1, Pallas kernels, local_partials(): pl.pallas_call(partials, out_shape=jax.ShapeDtypeStruct((32 * ROWS, 128),...  2.6 us
  transfers between devices with their start and end apart: 4, of which 2 were waited for; matrix products, arithmetic and copies ran while one was open for 1% of the time, Pallas kernels for 30%

profile of v1, /device:TPU:1, one launch (start us, length us, event | category | flops | bytes accessed | tf_op | source)
XLA Modules:
  0.0 91.3 jit_solution(11798487204777932624)
XLA Ops:
  0.6 2.6 %partials.1 = f32[768,128]{1,0:T(8,128)} custom-call(s32[1]{0:T(128)} %bitcast.tm_ref, f32[4,512]{1,0:T(4,128)} %obs_ref.1, bf16[512,512]{1,0:T(8,128)(2,1)} %load_ref.1, f32[1,512]{1,0:T(1,128)} %bitcast.10), custom_call_target="tpu_custom_call" | custom-call | tf_op jit(solution)/shard_map/partials/pallas_call | solution.py:294
  3.2 10.5 %all-to-all-start = ((f32[32,24,128]{2,1,0:T(8,128)}), f32[32,24,128]{2,1,0:T(8,128)S(1)}, u32[]{:S(2)}, u32[]{:S(2)}) async-start(f32[32,24,128]{2,1,0:T(8,128)} %bitcast.8), calls=%async_computation | async-start | bytes 786432 | tf_op jit(solution)/shard_map/all_to_all | solution.py:309
  13.7 11.0 %prep_a.1 = (f32[512,512]{1,0:T(8,128)}, f32[512,512]{1,0:T(8,128)}, f32[512,512]{1,0:T(8,128)}) custom-call(f32[512,512]{1,0:T(8,128)} %dyn_ref, f32[512,512]{1,0:T(8,128)} %prior_ref.2), custom_call_target="tpu_custom_call" | custom-call | tf_op jit(solution)/shard_map/prep_a/pallas_call | solution.py:265
  24.7 2.8 %all-to-all-done.in_ref = f32[32,24,128]{2,1,0:T(8,128)S(1)} async-done(((f32[32,24,128]{2,1,0:T(8,128)}), f32[32,24,128]{2,1,0:T(8,128)S(1)}, u32[]{:S(2)}, u32[]{:S(2)}) %all-to-all-start) | async-done | bytes 393248 | tf_op jit(solution)/shard_map/all_to_all | solution.py:309
  27.5 0.0 copy-start.1
  27.6 0.8 copy-done.1
  28.3 1.8 %sum_and_spread.1 = f32[32,24,128]{2,1,0:T(8,128)} custom-call(f32[32,24,128]{2,1,0:T(8,128)} %copy-done.1), custom_call_target="tpu_custom_call" | custom-call | tf_op jit(solution)/shard_map/sum_and_spread/pallas_call | solution.py:303
  30.1 6.4 %all-to-all-start.1 = ((f32[32,24,128]{2,1,0:T(8,128)}), f32[32,24,128]{2,1,0:T(8,128)S(1)}, u32[]{:S(2)}, u32[]{:S(2)}) async-start(f32[32,24,128]{2,1,0:T(8,128)} %sum_and_spread.1), calls=%async_computation.1 | async-start | bytes 786432 | tf_op jit(solution)/shard_map/all_to_all | solution.py:309
  36.5 5.9 %prep_b.1.pinv_ref = f32[512,512]{1,0:T(8,128)} custom-call(f32[512,512]{1,0:T(8,128)} %prior_ref.2, f32[512,512]{1,0:T(8,128)} %get-tuple-element.20.x_in), custom_call_target="tpu_custom_call" | custom-call | tf_op jit(solution)/shard_map/prep_b/pallas_call | solution.py:269
  42.4 7.3 %all-to-all-done.1 = f32[32,24,128]{2,1,0:T(8,128)S(1)} async-done(((f32[32,24,128]{2,1,0:T(8,128)}), f32[32,24,128]{2,1,0:T(8,128)S(1)}, u32[]{:S(2)}, u32[]{:S(2)}) %all-to-all-start.1) | async-done | bytes 393248 | tf_op jit(solution)/shard_map/all_to_all | solution.py:309
  49.7 0.0 copy-start
  49.7 5.1 %collective-permute-start = (f32[768,128]{1,0:T(8,128)S(1)}, f32[768,128]{1,0:T(8,128)S(1)}, u32[]{:S(2)}, u32[]{:S(2)}) collective-permute-start(f32[768,128]{1,0:T(8,128)S(1)} %bitcast.5), channel_id=1, source_target_pairs={{0,1},{1,0},{2,3},{3,2},{4,5},{5,4},{6,7},{7,6},{8,9},{9,8},{10,11... | collective-permute-start | bytes 1179656 | tf_op jit(solution)/shard_map/ppermute | solution.py:323
  54.8 0.7 broadcast_in_dim.3
  55.5 10.4 %all-to-all-start.2 = ((f32[16,16,128]{2,1,0:T(8,128)}), f32[16,16,128]{2,1,0:T(8,128)S(1)}, u32[]{:S(2)}, u32[]{:S(2)}) async-start(f32[16,16,128]{2,1,0:T(8,128)} %broadcast_in_dim.3), calls=%async_computation.2 | async-start | bytes 262144 | tf_op jit(solution)/shard_map/all_to_all | solution.py:309
  65.9 0.0 collective-permute-done.other_ref
  65.9 0.0 copy-start.3
  65.9 0.0 copy-done
  65.9 0.7 copy-done.3
  66.7 10.0 %invert.1 = (f32[512,512]{1,0:T(8,128)}, f32[512,512]{1,0:T(8,128)}, f32[512,512]{1,0:T(8,128)}) custom-call(s32[1]{0:T(128)} %bitcast.tm_ref, f32[768,128]{1,0:T(8,128)} %bitcast.7, f32[768,128]{1,0:T(8,128)} %copy-done.3, f32[512,512]{1,0:T(8,128)} %prior_ref.2, f32[512,512]{1,0:T(8,128)} %prep_b.1.pinv_ref, f32[512,512]{1,0:T(8,128)} %get-tuple-element.23.wt_ref), custom_call_target="tpu_custom_call" | custom-call | tf_op jit(solution)/shard_map/invert/pallas_call | solution.py:273
  76.7 0.0 all-to-all-done.2
  76.7 0.0 copy-start.2
  76.7 0.6 copy-done.2
  77.4 13.9 %scans.1 = (f32[4,512]{1,0:T(4,128)}, f32[4,512]{1,0:T(4,128)}) custom-call(s32[1]{0:T(128)} %bitcast.tm_ref, f32[256,128]{1,0:T(8,128)} %bitcast.9, f32[512,512]{1,0:T(8,128)} %get-tuple-element.24.x_ref, f32[512,512]{1,0:T(8,128)} %get-tuple-element.25.ft_ref, f32[512,512]{1,0:T(8,128)} %get-tuple-element.26.a_ref, f32[512,512]{1,0:T(8,128)} %get-tuple-element.27.nn_ref), custom_call_target="tpu_custom_call" | custom-call | tf_op jit(solution)/shard_map/scans/pallas_call | solution.py:284
  (1 shorter events, 0.0 us)
Async XLA Ops:
  3.2 24.3 %all-to-all-start = ((f32[32,24,128]{2,1,0:T(8,128)}), f32[32,24,128]{2,1,0:T(8,128)S(1)}, u32[]{:S(2)}, u32[]{:S(2)}) async-start(f32[32,24,128]{2,1,0:T(8,128)} %bitcast.8), calls=%async_computation | async-start | bytes 786432 | tf_op jit(solution)/shard_map/all_to_all | solution.py:309
  27.5 0.8 copy-start.1
  30.1 19.6 %all-to-all-start.1 = ((f32[32,24,128]{2,1,0:T(8,128)}), f32[32,24,128]{2,1,0:T(8,128)S(1)}, u32[]{:S(2)}, u32[]{:S(2)}) async-start(f32[32,24,128]{2,1,0:T(8,128)} %sum_and_spread.1), calls=%async_computation.1 | async-start | bytes 786432 | tf_op jit(solution)/shard_map/all_to_all | solution.py:309
  49.7 16.2 %copy-start = (f32[32,24,128]{2,1,0:T(8,128)}, f32[32,24,128]{2,1,0:T(8,128)S(1)}, u32[]{:S(2)}) copy-start(f32[32,24,128]{2,1,0:T(8,128)S(1)} %all-to-all-done.1) | copy-start | bytes 1179652
  49.7 16.2 %collective-permute-start = (f32[768,128]{1,0:T(8,128)S(1)}, f32[768,128]{1,0:T(8,128)S(1)}, u32[]{:S(2)}, u32[]{:S(2)}) collective-permute-start(f32[768,128]{1,0:T(8,128)S(1)} %bitcast.5), channel_id=1, source_target_pairs={{0,1},{1,0},{2,3},{3,2},{4,5},{5,4},{6,7},{7,6},{8,9},{9,8},{10,11... | collective-permute-start | bytes 1179656 | tf_op jit(solution)/shard_map/ppermute | solution.py:323
  55.5 21.3 %all-to-all-start.2 = ((f32[16,16,128]{2,1,0:T(8,128)}), f32[16,16,128]{2,1,0:T(8,128)S(1)}, u32[]{:S(2)}, u32[]{:S(2)}) async-start(f32[16,16,128]{2,1,0:T(8,128)} %broadcast_in_dim.3), calls=%async_computation.2 | async-start | bytes 262144 | tf_op jit(solution)/shard_map/all_to_all | solution.py:309
  65.9 0.8 copy-start.3
  76.7 0.6 copy-start.2

commit v2 on v1

--- a/solution.py
+++ b/solution.py
@@ -101,14 +101,6 @@
         for c in range(4):
             out_ref[INFO + 4 * t + c : INFO + 4 * t + c + 1, :] = info[t : t + 1, 128 * c : 128 * c + 128]
     out_ref[INFO + 16 :, :] = jnp.zeros((32 * ROWS - INFO - 16, 128), f32)
-
-
-def sum_and_spread(in_ref, out_ref):
-    total = in_ref[0]
-    for n in range(1, 32):
-        total = total + in_ref[n]
-    for n in range(32):
-        out_ref[n] = total
 
 
 def prep_a(dyn_ref, prior_ref, wt_ref, nn_ref, x_ref):
@@ -135,7 +127,7 @@
     lax.fori_loop(0, 6, body, 0)
 
 
-def refine(times_mat, x_ref, r_ref, done2, cap):
+def refine(times_mat, x_ref, r_ref, done2, cap, product):
     ident = eye()
 
     def residual():
@@ -150,27 +142,58 @@
     def body(c):
         k, n2, _ = c
         x = x_ref[...]
-        x_ref[...] = x + dot3(split(x), split(r_ref[...]))
+        x_ref[...] = x + product(x, r_ref[...])
         return k + 1, residual(), n2
 
     n0 = residual()
-    return lax.while_loop(cond, body, (jnp.int32(0), n0, jnp.float32(jnp.inf)))
-
-
-def prep_b(prior_ref, x_in, x_ref, r_ref):
+    return lax.while_loop(cond, body, (jnp.int32(0), n0, jnp.float32(jnp.inf)))[1]
+
+
+def coarse(a, b):
+    return dot1(a.astype(bf16), b.astype(bf16))
+
+
+def fine(a, b):
+    return dot3(split(a), split(b))
+
+
+def prep_b(prior_ref, dyn_ref, x_in, x_ref, rest_ref, wp_ref, r_ref):
     x_ref[...] = x_in[...]
-    _, n2, _ = refine(lambda v: dot3(split(prior_ref[...]), split(v)), x_ref, r_ref, 1e-5, 40)
-
-    @pl.when(jnp.logical_not(n2 < 0.05))
+    n2 = refine(lambda v: fine(prior_ref[...], v), x_ref, r_ref, 1e-5, 40, coarse)
+
+    @pl.when(jnp.logical_not(n2 < 1e-3))
     def _():
-        x_ref[...] = prior_ref[...]
-        sweep_inverse(x_ref)
+        x_ref[...] = x_in[...]
+        n2 = refine(lambda v: dot6(prior_ref[...], v), x_ref, r_ref, 1e-5, 40, fine)
+
+        @pl.when(jnp.logical_not(n2 < 1e-2))
+        def _():
+            x_ref[...] = prior_ref[...]
+            sweep_inverse(x_ref)
+
+    rest = eye() - dot6(prior_ref[...], x_ref[...])
+    rest_ref[...] = rest
+    turned = dyn_ref[...].T
+    wp_ref[...] = turned - coarse(turned, rest)
 
 
 PAIRS = ((0, 0), (0, 1), (0, 2), (0, 3), (1, 1), (1, 2), (1, 3), (2, 2), (2, 3), (3, 3))
 
 
-def invert(tm_ref, own_ref, other_ref, prior_ref, pinv_ref, wt_ref, a_ref, x_ref, ft_ref, g_ref, r_ref):
+def copies(sources, targets, sems):
+    return [pltpu.make_async_copy(a, b, sems.at[n]) for n, (a, b) in enumerate(zip(sources, targets))]
+
+
+def invert(tm_ref, *refs):
+    sources, results, held, made, (g_ref, r_ref, sems, out_sems) = refs[:8], refs[8:11], refs[11:19], refs[19:22], refs[22:]
+    own_ref, other_ref, pinv_ref, rest_ref, wp_ref, prior_ref, nn_ref, wt_ref = held
+    x_ref, ft_ref, m_ref = made
+    loads = copies(sources, held, sems)
+    stores = copies(made, results, out_sems)
+    for c in loads:
+        c.start()
+    loads[0].wait()
+    loads[1].wait()
     first = lax.rem(tm_ref[0], 2) == 0
     for n, (i, j) in enumerate(PAIRS):
         at = (n % 5) * 128
@@ -180,43 +203,56 @@
         if i != j:
             g_ref[128 * j : 128 * j + 128, 128 * i : 128 * i + 128] = blk.T
     gram = g_ref[...]
-    a = prior_ref[...] + gram
-    a_ref[...] = a
-    pinv = pinv_ref[...]
-    ph = pinv.astype(bf16)
-    e = dot1(gram.astype(bf16), ph)
-    size = jnp.sqrt(sum_sq(e))
-    theta = jnp.where(size < 0.9, 1.0, 2.0 / (2.0 + size))
-    r0 = (1.0 - theta) * eye() - theta * e
-    rh = r0.astype(bf16)
-    t = dot1(rh, rh)
-    s = r0 + t + dot1(rh, t.astype(bf16))
-    x_ref[...] = theta * (pinv + dot1(ph, s.astype(bf16)))
-    _, n2, _ = refine(lambda v: dot6(a_ref[...], v), x_ref, r_ref, 1e-4, 60)
-
-    good = n2 < 1e-4
-
-    @pl.when(good)
+    loads[2].wait()
+    loads[3].wait()
+    psplit = split(pinv_ref[...])
+    h = dot3(split(gram), psplit) - rest_ref[...]
+    hs = split(h)
+    t = dot1(hs[0], hs[0])
+    s = t - h - dot1(hs[0], t.astype(bf16))
+    ss = split(s)
+    r = -(h + s + dot3(hs, ss))
+    n2 = sum_sq(r)
+    rh = r.astype(bf16)
+    r = r + dot1(rh, rh)
+    s = s + r + dot1(ss[0], r.astype(bf16))
+    ss = split(s)
+    for c in loads[4:]:
+        c.wait()
+    m_ref[...] = gram + (prior_ref[...] - nn_ref[...])
+    stores[2].start()
+    wp = wp_ref[...]
+    x_ref[...] = pinv_ref[...] + dot3(psplit, ss)
+    ft_ref[...] = wp + dot3(split(wp), ss)
+
+    @pl.when(jnp.logical_not(n2 < 1e-4))
     def _():
-        x = x_ref[...]
-        r = r_ref[...]
-        rh = r.astype(bf16)
-        x_ref[...] = x + dot1(x.astype(bf16), (r + dot1(rh, rh)).astype(bf16))
-
-    @pl.when(jnp.logical_not(good))
-    def _():
-        x_ref[...] = a_ref[...]
-        sweep_inverse(x_ref)
-
-    ft_ref[...] = dot6(wt_ref[...], x_ref[...])
-
-
-def scans(tm_ref, info_ref, x_ref, ft_ref, a_ref, nn_ref, filt_ref, smooth_ref, f_ref, s_ref):
+        e = coarse(g_ref[...], pinv_ref[...])
+        theta = 2.0 / (2.0 + jnp.sqrt(sum_sq(e)))
+        x_ref[...] = theta * pinv_ref[...]
+        n2 = refine(lambda v: dot6(prior_ref[...] + g_ref[...], v), x_ref, r_ref, 1e-9, 60, fine)
+
+        @pl.when(jnp.logical_not(n2 < 1e-6))
+        def _():
+            x_ref[...] = prior_ref[...] + g_ref[...]
+            sweep_inverse(x_ref)
+
+        ft_ref[...] = dot6(wt_ref[...], x_ref[...])
+
+    stores[0].start()
+    stores[1].start()
+    for c in stores:
+        c.wait()
+
+
+def scans(tm_ref, *refs):
+    sources, (filt_ref, smooth_ref), held, (f_ref, s_ref, sems) = refs[:5], refs[5:7], refs[7:12], refs[12:]
+    ft_ref, info_ref, x_ref, m_ref, nn_ref = held
+    loads = copies(sources, held, sems)
+    for c in loads:
+        c.start()
     T = 64
-    x = split(x_ref[...])
-    parts = [info_ref[pl.ds(c, T, stride=4), :] for c in range(4)]
-    info = jnp.concatenate(parts, axis=1)
-    y = dot3(split(info), x)
+    loads[0].wait()
     f = ft_ref[...]
     powers = [split(f)]
     ident = eye()
@@ -225,6 +261,12 @@
     es = split(e)
     f = c * (f + e) + dot3(es, es)
     powers.append(split(f))
+    loads[1].wait()
+    loads[2].wait()
+    x = split(x_ref[...])
+    parts = [info_ref[pl.ds(c, T, stride=4), :] for c in range(4)]
+    info = jnp.concatenate(parts, axis=1)
+    y = dot3(split(info), x)
     for _ in range(4):
         f = dot3(powers[-1], powers[-1])
         powers.append(split(f))
@@ -239,9 +281,11 @@
     for n, p in enumerate(powers):
         y = y + later(dot3(split(y), p), 1 << n)
     f_ref[...] = y
+    loads[3].wait()
+    loads[4].wait()
     nn = nn_ref[...]
     ys = split(y)
-    u = dot3(ys, split(a_ref[...] - nn))
+    u = dot3(ys, split(m_ref[...]))
     tail = dot3(split(y[T - 8 :, :]), split(nn))
     u = u + jnp.where(step == T - 1, jnp.concatenate([jnp.zeros((T - 8, R), f32), tail], axis=0), 0.0)
     for n, p in enumerate(powers):
@@ -255,39 +299,55 @@
     smooth_ref[...] = jnp.where(half, sb[0:4], sb[4:8])
 
 
-vm = partial(pltpu.VMEM, (R, R))
+vm = partial(pltpu.VMEM, (R, R), f32)
 mat = jax.ShapeDtypeStruct((R, R), f32)
 smem = pl.BlockSpec(memory_space=pltpu.SMEM)
 vmem = pl.BlockSpec(memory_space=pltpu.VMEM)
+room = pltpu.CompilerParams(vmem_limit_bytes=28 << 20)
+
+
+anywhere = pl.BlockSpec(memory_space=pl.ANY)
+far = pltpu.HBM((R, R), f32)
+
+
+def kept_far(arrays):
+    return [pltpu.with_memory_space_constraint(a, pltpu.HBM) for a in arrays]
+
+part = pltpu.VMEM((32 * ROWS, 128), f32)
 
 
 def prep_first(dyn, prior):
     return pl.pallas_call(prep_a, out_shape=(mat, mat, mat), name="prep_a")(dyn, prior)
 
 
-def prep_second(prior, x):
-    return pl.pallas_call(prep_b, out_shape=mat, scratch_shapes=[vm(f32)], name="prep_b")(prior, x)
-
-
-def inverse(tm, own, other, prior, pinv, wt):
+def prep_second(prior, dyn, x):
+    return pl.pallas_call(prep_b, out_shape=(mat, mat, mat), scratch_shapes=[vm()], name="prep_b")(prior, dyn, x)
+
+
+def inverse(tm, *arrays):
+    dma = pltpu.SemaphoreType.DMA
     return pl.pallas_call(
         invert,
-        out_shape=(mat, mat, mat),
-        in_specs=[smem] + [vmem] * 5,
-        scratch_shapes=[vm(f32), vm(f32)],
+        out_shape=(far, far, far),
+        in_specs=[smem] + [anywhere] * 8,
+        out_specs=(anywhere,) * 3,
+        scratch_shapes=[part, part] + [vm()] * 11 + [dma((8,)), dma((3,))],
         name="invert",
-    )(tm, own, other, prior, pinv, wt)
-
-
-def time_scans(tm, info, x, ft, a, nn):
+        compiler_params=room,
+    )(tm, *arrays[:2], *kept_far(arrays[2:]))
+
+
+def time_scans(tm, *arrays):
     out = jax.ShapeDtypeStruct((4, R), f32)
+    rows = pltpu.VMEM((64, R), f32)
     return pl.pallas_call(
         scans,
         out_shape=(out, out),
-        in_specs=[smem] + [vmem] * 5,
-        scratch_shapes=[pltpu.VMEM((64, R), f32)] * 2,
+        in_specs=[smem] + [anywhere] * 5,
+        scratch_shapes=[vm(), pltpu.VMEM((256, 128), f32), vm(), vm(), vm(), rows, rows, pltpu.SemaphoreType.DMA((5,))],
         name="scans",
-    )(tm, info, x, ft, a, nn)
+        compiler_params=room,
+    )(tm, *kept_far(arrays[:1]), arrays[1], *kept_far(arrays[2:]))
 
 
 def local_partials(tm, observed, loadings, noise):
@@ -299,12 +359,6 @@
     )(tm, observed, loadings, noise)
 
 
-def summed(pieces):
-    return pl.pallas_call(
-        sum_and_spread, out_shape=jax.ShapeDtypeStruct(pieces.shape, f32), name="sum_and_spread"
-    )(pieces)
-
-
 def exchange(pieces, axis):
     return lax.all_to_all(pieces, axis, split_axis=0, concat_axis=0, tiled=True)
 
@@ -315,16 +369,16 @@
     send, dynamics, prior_prec = lax.optimization_barrier((send, dynamics, prior_prec))
     pieces = exchange(send.reshape(32, ROWS, 128), "sens")
     wt, nn, x0 = prep_first(dynamics, prior_prec)
-    total = summed(pieces)
+    total = jnp.broadcast_to(pieces.sum(axis=0), pieces.shape)
     total, x0 = lax.optimization_barrier((total, x0))
     own = exchange(total, "sens").reshape(32 * ROWS, 128)
-    pinv = prep_second(prior_prec, x0)
+    pinv, rest, wp = prep_second(prior_prec, dynamics, x0)
     own, pinv = lax.optimization_barrier((own, pinv))
     other = lax.ppermute(own, "tm", [(i, i ^ 1) for i in range(16)])
     info = jnp.broadcast_to(own[INFO : INFO + 16], (16, 16, 128))
     info = exchange(info, "tm").reshape(256, 128)
-    a, x, ft = inverse(tm, own, other, prior_prec, pinv, wt)
-    return time_scans(tm, info, x, ft, a, nn)
+    x, ft, m = inverse(tm, own, other, pinv, rest, wp, prior_prec, nn, wt)
+    return time_scans(tm, ft, info, x, m, nn)
 
 
 def solution(mesh):

time: 91.8 us -> 87.3 us (0.951)
  waiting for transfers between devices: 10.1 us -> 7.85 us
  local copies, waits for them, and re-layouts: 2.82 us -> 1.42 us
  Pallas kernels: 45.3 us -> 44.2 us
    all_to_all x3, waiting for transfers between devices: 10.1 us -> 7.85 us  [exchange(): return lax.all_to_all(pieces, axis, split_axis=0, concat_axis=0, tiled=True)]
    unnamed x8 -> x0, local copies, waits for them, and re-layouts: 2.15 us -> none
    pallas_call x4 -> x3, Pallas kernels: 31.7 us -> 30.6 us  [the longest x1 13.4 us: time_scans(): pl.pallas_call(scans, out_shape=(out, out), in_specs=[smem] + [anywhere]...]
  transfers between devices with their start and end apart: 4 -> 4, of which waited for: 2 -> 2; matrix products, arithmetic and copies ran while one was open for 1% -> 1% of each run, Pallas kernels for 30% -> 32%
where the time goes in v2:
time: 87.3 us; the launch traced here: 86.8 us
  Pallas kernels  44.2 us (51%)
  starting transfers between devices  32.4 us (37%)
  waiting for transfers between devices  7.85 us (9%)
  local copies, waits for them, and re-layouts  1.42 us (2%)
  between operations  0.89 us (1%)
    all_to_all x3, starting transfers between devices, exchange(): return lax.all_to_all(pieces, axis, split_axis=0, concat_axis=0, tiled=True)  27.4 us
    pallas_call x1, Pallas kernels, time_scans(): pl.pallas_call(scans, out_shape=(out, out), in_specs=[smem] + [anywhere]...  13.4 us
    pallas_call x1, Pallas kernels, prep_first(): pl.pallas_call(prep_a, out_shape=(mat, mat, mat), name='prep_a')(dyn, prior)  11 us
    pallas_call x1, Pallas kernels, inverse(): pl.pallas_call(invert, out_shape=(far, far, far), in_specs=[smem] + [anyw...  9.03 us
    pallas_call x1, Pallas kernels, prep_second(): pl.pallas_call(prep_b, out_shape=(mat, mat, mat), scratch_shapes=[vm()],...  8.15 us
    all_to_all x3, waiting for transfers between devices, exchange(): return lax.all_to_all(pieces, axis, split_axis=0, concat_axis=0, tiled=True)  7.85 us
    ppermute x1, starting transfers between devices, shards(): other = lax.ppermute(own, 'tm', [(i, i ^ 1) for i in range(16)])  5.09 us
    pallas_call x1, Pallas kernels, local_partials(): pl.pallas_call(partials, out_shape=jax.ShapeDtypeStruct((32 * ROWS, 128),...  2.59 us
  transfers between devices with their start and end apart: 4, of which 2 were waited for; matrix products, arithmetic and copies ran while one was open for 1% of the time, Pallas kernels for 32%

profile of v2, /device:TPU:1, one launch (start us, length us, event | category | flops | bytes accessed | tf_op | source)
XLA Modules:
  0.0 86.8 jit_solution(4624909298642920331)
XLA Ops:
  0.6 2.6 %partials.1 = f32[768,128]{1,0:T(8,128)} custom-call(s32[1]{0:T(128)} %bitcast.tm_ref, f32[4,512]{1,0:T(4,128)} %obs_ref.1, bf16[512,512]{1,0:T(8,128)(2,1)} %load_ref.1, f32[1,512]{1,0:T(1,128)} %bitcast.10), custom_call_target="tpu_custom_call" | custom-call | tf_op jit(solution)/shard_map/partials/pallas_call | solution.py:354
  3.2 10.5 %all-to-all-start = ((f32[32,24,128]{2,1,0:T(8,128)}), f32[32,24,128]{2,1,0:T(8,128)S(1)}, u32[]{:S(2)}, u32[]{:S(2)}) async-start(f32[32,24,128]{2,1,0:T(8,128)} %bitcast.9), calls=%async_computation | async-start | bytes 786432 | tf_op jit(solution)/shard_map/all_to_all | solution.py:363
  13.7 11.0 %prep_a.1 = (f32[512,512]{1,0:T(8,128)}, f32[512,512]{1,0:T(8,128)}, f32[512,512]{1,0:T(8,128)}) custom-call(f32[512,512]{1,0:T(8,128)} %dyn_ref.1, f32[512,512]{1,0:T(8,128)} %refs_5_), custom_call_target="tpu_custom_call" | custom-call | tf_op jit(solution)/shard_map/prep_a/pallas_call | solution.py:320
  24.7 2.8 %all-to-all-done = f32[32,24,128]{2,1,0:T(8,128)S(1)} async-done(((f32[32,24,128]{2,1,0:T(8,128)}), f32[32,24,128]{2,1,0:T(8,128)S(1)}, u32[]{:S(2)}, u32[]{:S(2)}) %all-to-all-start) | async-done | bytes 393248 | tf_op jit(solution)/shard_map/all_to_all | solution.py:363
  27.6 0.8 broadcast_in_dim.6
  28.4 6.4 %all-to-all-start.1 = ((f32[32,24,128]{2,1,0:T(8,128)}), f32[32,24,128]{2,1,0:T(8,128)S(1)}, u32[]{:S(2)}, u32[]{:S(2)}) async-start(f32[32,24,128]{2,1,0:T(8,128)} %broadcast_in_dim.6), calls=%async_computation.1 | async-start | bytes 786432 | tf_op jit(solution)/shard_map/all_to_all | solution.py:363
  34.8 8.2 %prep_b.1 = (f32[512,512]{1,0:T(8,128)}, f32[512,512]{1,0:T(8,128)}, f32[512,512]{1,0:T(8,128)}) custom-call(f32[512,512]{1,0:T(8,128)} %refs_5_, f32[512,512]{1,0:T(8,128)} %dyn_ref.1, f32[512,512]{1,0:T(8,128)} %get-tuple-element.23.x_in), custom_call_target="tpu_custom_call" | custom-call | tf_op jit(solution)/shard_map/prep_b/pallas_call | solution.py:324
  42.9 5.0 %all-to-all-done.1 = f32[32,24,128]{2,1,0:T(8,128)S(1)} async-done(((f32[32,24,128]{2,1,0:T(8,128)}), f32[32,24,128]{2,1,0:T(8,128)S(1)}, u32[]{:S(2)}, u32[]{:S(2)}) %all-to-all-start.1) | async-done | bytes 393248 | tf_op jit(solution)/shard_map/all_to_all | solution.py:363
  48.0 5.1 %collective-permute-start = (f32[768,128]{1,0:T(8,128)S(1)}, f32[768,128]{1,0:T(8,128)S(1)}, u32[]{:S(2)}, u32[]{:S(2)}) collective-permute-start(f32[768,128]{1,0:T(8,128)S(1)} %bitcast.5), channel_id=1, source_target_pairs={{0,1},{1,0},{2,3},{3,2},{4,5},{5,4},{6,7},{7,6},{8,9},{9,8},{10,11... | collective-permute-start | bytes 1179656 | tf_op jit(solution)/shard_map/ppermute | solution.py:377
  53.1 0.6 broadcast_in_dim.7
  53.7 10.5 %all-to-all-start.2 = ((f32[16,16,128]{2,1,0:T(8,128)}), f32[16,16,128]{2,1,0:T(8,128)S(1)}, u32[]{:S(2)}, u32[]{:S(2)}) async-start(f32[16,16,128]{2,1,0:T(8,128)} %broadcast_in_dim.7), calls=%async_computation.2 | async-start | bytes 262144 | tf_op jit(solution)/shard_map/all_to_all | solution.py:363
  64.2 0.0 collective-permute-done.refs_1_
  64.2 9.0 %invert.1 = (f32[512,512]{1,0:T(8,128)}, f32[512,512]{1,0:T(8,128)}, f32[512,512]{1,0:T(8,128)}) custom-call(s32[1]{0:T(128)} %bitcast.tm_ref, f32[768,128]{1,0:T(8,128)S(1)} %bitcast.7, f32[768,128]{1,0:T(8,128)S(1)} %collective-permute-done.refs_1_, f32[512,512]{1,0:T(8,128)} %get-tuple-element.26.refs_2_, f32[512,512]{1,0:T(8,128)} %get-tuple-element.27.refs_3_, ...), custom_call_target="tpu_custom_call" | custom-call | tf_op jit(solution)/shard_map/invert/pallas_call | solution.py:329
  73.2 0.0 all-to-all-done.2
  73.2 13.4 %scans.1 = (f32[4,512]{1,0:T(4,128)}, f32[4,512]{1,0:T(4,128)}) custom-call(s32[1]{0:T(128)} %bitcast.tm_ref, f32[512,512]{1,0:T(8,128)} %get-tuple-element.31.refs_0_, f32[256,128]{1,0:T(8,128)S(1)} %bitcast.8, f32[512,512]{1,0:T(8,128)} %get-tuple-element.32.refs_2_, f32[512,512]{1,0:T(8,128)} %get-tuple-element.33.refs_3_, ...), custom_call_target="tpu_custom_call" | custom-call | tf_op jit(solution)/shard_map/scans/pallas_call | solution.py:343
  (2 shorter events, 0.0 us)
Async XLA Ops:
  3.2 24.3 %all-to-all-start = ((f32[32,24,128]{2,1,0:T(8,128)}), f32[32,24,128]{2,1,0:T(8,128)S(1)}, u32[]{:S(2)}, u32[]{:S(2)}) async-start(f32[32,24,128]{2,1,0:T(8,128)} %bitcast.9), calls=%async_computation | async-start | bytes 786432 | tf_op jit(solution)/shard_map/all_to_all | solution.py:363
  28.4 19.6 %all-to-all-start.1 = ((f32[32,24,128]{2,1,0:T(8,128)}), f32[32,24,128]{2,1,0:T(8,128)S(1)}, u32[]{:S(2)}, u32[]{:S(2)}) async-start(f32[32,24,128]{2,1,0:T(8,128)} %broadcast_in_dim.6), calls=%async_computation.1 | async-start | bytes 786432 | tf_op jit(solution)/shard_map/all_to_all | solution.py:363
  48.0 16.2 %collective-permute-start = (f32[768,128]{1,0:T(8,128)S(1)}, f32[768,128]{1,0:T(8,128)S(1)}, u32[]{:S(2)}, u32[]{:S(2)}) collective-permute-start(f32[768,128]{1,0:T(8,128)S(1)} %bitcast.5), channel_id=1, source_target_pairs={{0,1},{1,0},{2,3},{3,2},{4,5},{5,4},{6,7},{7,6},{8,9},{9,8},{10,11... | collective-permute-start | bytes 1179656 | tf_op jit(solution)/shard_map/ppermute | solution.py:377
  53.7 19.5 %all-to-all-start.2 = ((f32[16,16,128]{2,1,0:T(8,128)}), f32[16,16,128]{2,1,0:T(8,128)S(1)}, u32[]{:S(2)}, u32[]{:S(2)}) async-start(f32[16,16,128]{2,1,0:T(8,128)} %broadcast_in_dim.7), calls=%async_computation.2 | async-start | bytes 262144 | tf_op jit(solution)/shard_map/all_to_all | solution.py:363

commit v3 on v2

--- a/solution.py
+++ b/solution.py
@@ -23,6 +23,12 @@
 
 def dot3(a, b, ca=1, cb=0):
     return dot1(a[0], b[0], ca, cb) + (dot1(a[0], b[1], ca, cb) + dot1(a[1], b[0], ca, cb))
+
+
+def rows3(a, b, ca=1, cb=0):
+    n = a[0].shape[0]
+    both = dot1(jnp.concatenate(a, axis=0), b[0], ca, cb)
+    return both[:n] + (both[n:] + dot1(a[0], b[1], ca, cb))
 
 
 def dot6(a, b, ca=1, cb=0):
@@ -103,12 +109,14 @@
     out_ref[INFO + 16 :, :] = jnp.zeros((32 * ROWS - INFO - 16, 128), f32)
 
 
-def prep_a(dyn_ref, prior_ref, wt_ref, nn_ref, x_ref):
+def prep_a(dyn_ref, prior_ref, wt_ref, nn_ref, q_ref, x_ref):
     prior = prior_ref[...]
     psplit = split(prior)
     wt = dot6(dyn_ref[...], prior, 0, 0)
     wt_ref[...] = wt
-    nn_ref[...] = dot6(wt, dyn_ref[...])
+    nn = dot6(wt, dyn_ref[...])
+    nn_ref[...] = nn
+    q_ref[...] = prior - nn
     col = jnp.sum(jnp.abs(prior), axis=0, keepdims=True)
     start = 1.0 / jnp.max(col, axis=1, keepdims=True)
     ident = eye()
@@ -172,7 +180,7 @@
             sweep_inverse(x_ref)
 
     rest = eye() - dot6(prior_ref[...], x_ref[...])
-    rest_ref[...] = rest
+    rest_ref[...] = rest.astype(bf16)
     turned = dyn_ref[...].T
     wp_ref[...] = turned - coarse(turned, rest)
 
@@ -186,11 +194,11 @@
 
 def invert(tm_ref, *refs):
     sources, results, held, made, (g_ref, r_ref, sems, out_sems) = refs[:8], refs[8:11], refs[11:19], refs[19:22], refs[22:]
-    own_ref, other_ref, pinv_ref, rest_ref, wp_ref, prior_ref, nn_ref, wt_ref = held
+    own_ref, other_ref, pinv_ref, rest_ref, wp_ref, q_ref, prior_ref, wt_ref = held
     x_ref, ft_ref, m_ref = made
     loads = copies(sources, held, sems)
     stores = copies(made, results, out_sems)
-    for c in loads:
+    for c in loads[:4]:
         c.start()
     loads[0].wait()
     loads[1].wait()
@@ -205,28 +213,37 @@
     gram = g_ref[...]
     loads[2].wait()
     loads[3].wait()
+    loads[4].start()
+    loads[5].start()
     psplit = split(pinv_ref[...])
-    h = dot3(split(gram), psplit) - rest_ref[...]
-    hs = split(h)
-    t = dot1(hs[0], hs[0])
-    s = t - h - dot1(hs[0], t.astype(bf16))
+    h = dot3(split(gram), psplit) - rest_ref[...].astype(f32)
+    h0, h1 = split(h)
+    r = (h0.astype(f32) - h) + (dot1(h0, h0) + dot1(h1, h0))
+    rh = r.astype(bf16)
+    rr = dot1(rh, rh)
+    n4 = sum_sq(rr)
+    r = r + rr + dot1(rh, rr.astype(bf16))
+    s = r - h0.astype(f32) - dot1(h0, r.astype(bf16))
     ss = split(s)
-    r = -(h + s + dot3(hs, ss))
-    n2 = sum_sq(r)
-    rh = r.astype(bf16)
-    r = r + dot1(rh, rh)
-    s = s + r + dot1(ss[0], r.astype(bf16))
-    ss = split(s)
-    for c in loads[4:]:
-        c.wait()
-    m_ref[...] = gram + (prior_ref[...] - nn_ref[...])
+    loads[4].wait()
+    loads[5].wait()
+    m_ref[...] = gram + q_ref[...]
     stores[2].start()
     wp = wp_ref[...]
-    x_ref[...] = pinv_ref[...] + dot3(psplit, ss)
-    ft_ref[...] = wp + dot3(split(wp), ss)
-
-    @pl.when(jnp.logical_not(n2 < 1e-4))
+    good = n4 < 1e-6
+
+    @pl.when(good)
     def _():
+        x_ref[...] = pinv_ref[...] + dot3(psplit, ss)
+        stores[0].start()
+        ft_ref[...] = wp + dot3(split(wp), ss)
+        stores[1].start()
+
+    @pl.when(jnp.logical_not(good))
+    def _():
+        for c in loads[6:]:
+            c.start()
+            c.wait()
         e = coarse(g_ref[...], pinv_ref[...])
         theta = 2.0 / (2.0 + jnp.sqrt(sum_sq(e)))
         x_ref[...] = theta * pinv_ref[...]
@@ -238,9 +255,9 @@
             sweep_inverse(x_ref)
 
         ft_ref[...] = dot6(wt_ref[...], x_ref[...])
-
-    stores[0].start()
-    stores[1].start()
+        stores[0].start()
+        stores[1].start()
+
     for c in stores:
         c.wait()
 
@@ -266,10 +283,11 @@
     x = split(x_ref[...])
     parts = [info_ref[pl.ds(c, T, stride=4), :] for c in range(4)]
     info = jnp.concatenate(parts, axis=1)
-    y = dot3(split(info), x)
-    for _ in range(4):
+    y = rows3(split(info), x)
+    for _ in range(3):
         f = dot3(powers[-1], powers[-1])
         powers.append(split(f))
+    leap = powers.pop()
     step = lax.broadcasted_iota(jnp.int32, (T, 1), 0)
 
     def later(v, k):
@@ -279,18 +297,26 @@
         return jnp.where(step < T - k, pltpu.roll(v, T - k, 0), 0.0)
 
     for n, p in enumerate(powers):
-        y = y + later(dot3(split(y), p), 1 << n)
+        y = y + later(rows3(split(y), p), 1 << n)
+    blocks = [y[16 * b : 16 * b + 16] for b in range(4)]
+    for b in range(1, 4):
+        blocks[b] = blocks[b] + rows3(split(blocks[b - 1]), leap)
+    y = jnp.concatenate(blocks, axis=0)
     f_ref[...] = y
     loads[3].wait()
     loads[4].wait()
     nn = nn_ref[...]
     ys = split(y)
-    u = dot3(ys, split(m_ref[...]))
+    u = rows3(ys, split(m_ref[...]))
     tail = dot3(split(y[T - 8 :, :]), split(nn))
     u = u + jnp.where(step == T - 1, jnp.concatenate([jnp.zeros((T - 8, R), f32), tail], axis=0), 0.0)
     for n, p in enumerate(powers):
-        u = u + sooner(dot3(split(u), p, 1, 1), 1 << n)
-    s_ref[...] = dot3(split(u), x)
+        u = u + sooner(rows3(split(u), p, 1, 1), 1 << n)
+    blocks = [u[16 * b : 16 * b + 16] for b in range(4)]
+    for b in range(2, -1, -1):
+        blocks[b] = blocks[b] + rows3(split(blocks[b + 1]), leap, 1, 1)
+    u = jnp.concatenate(blocks, axis=0)
+    s_ref[...] = rows3(split(u), x)
     at = pl.multiple_of(8 * lax.div(tm_ref[0], 2), 8)
     half = lax.rem(tm_ref[0], 2) == 0
     fb = f_ref[pl.ds(at, 8), :]
@@ -301,6 +327,7 @@
 
 vm = partial(pltpu.VMEM, (R, R), f32)
 mat = jax.ShapeDtypeStruct((R, R), f32)
+half = jax.ShapeDtypeStruct((R, R), bf16)
 smem = pl.BlockSpec(memory_space=pltpu.SMEM)
 vmem = pl.BlockSpec(memory_space=pltpu.VMEM)
 room = pltpu.CompilerParams(vmem_limit_bytes=28 << 20)
@@ -317,11 +344,11 @@
 
 
 def prep_first(dyn, prior):
-    return pl.pallas_call(prep_a, out_shape=(mat, mat, mat), name="prep_a")(dyn, prior)
+    return pl.pallas_call(prep_a, out_shape=(mat,) * 4, name="prep_a")(dyn, prior)
 
 
 def prep_second(prior, dyn, x):
-    return pl.pallas_call(prep_b, out_shape=(mat, mat, mat), scratch_shapes=[vm()], name="prep_b")(prior, dyn, x)
+    return pl.pallas_call(prep_b, out_shape=(mat, half, mat), scratch_shapes=[vm()], name="prep_b")(prior, dyn, x)
 
 
 def inverse(tm, *arrays):
@@ -331,7 +358,7 @@
         out_shape=(far, far, far),
         in_specs=[smem] + [anywhere] * 8,
         out_specs=(anywhere,) * 3,
-        scratch_shapes=[part, part] + [vm()] * 11 + [dma((8,)), dma((3,))],
+        scratch_shapes=[part, part, vm(), pltpu.VMEM((R, R), bf16)] + [vm()] * 9 + [dma((8,)), dma((3,))],
         name="invert",
         compiler_params=room,
     )(tm, *arrays[:2], *kept_far(arrays[2:]))
@@ -368,7 +395,7 @@
     send = local_partials(tm, observed, loadings, noise_prec.reshape(1, R))
     send, dynamics, prior_prec = lax.optimization_barrier((send, dynamics, prior_prec))
     pieces = exchange(send.reshape(32, ROWS, 128), "sens")
-    wt, nn, x0 = prep_first(dynamics, prior_prec)
+    wt, nn, q, x0 = prep_first(dynamics, prior_prec)
     total = jnp.broadcast_to(pieces.sum(axis=0), pieces.shape)
     total, x0 = lax.optimization_barrier((total, x0))
     own = exchange(total, "sens").reshape(32 * ROWS, 128)
@@ -377,7 +404,7 @@
     other = lax.ppermute(own, "tm", [(i, i ^ 1) for i in range(16)])
     info = jnp.broadcast_to(own[INFO : INFO + 16], (16, 16, 128))
     info = exchange(info, "tm").reshape(256, 128)
-    x, ft, m = inverse(tm, own, other, pinv, rest, wp, prior_prec, nn, wt)
+    x, ft, m = inverse(tm, own, other, pinv, rest, wp, q, prior_prec, wt)
     return time_scans(tm, ft, info, x, m, nn)
 
 

time: 87.3 us -> 85.2 us (0.976)
  Pallas kernels: 44.2 us -> 40.6 us
  waiting for transfers between devices: 7.85 us -> 9.01 us
    pallas_call x1, Pallas kernels: 13.4 us -> 11.2 us  [time_scans(): pl.pallas_call(scans, out_shape=(out, out), in_specs=[smem] + [anywhere]...]
    pallas_call x1, Pallas kernels: 9.03 us -> 7.49 us  [inverse(): pl.pallas_call(invert, out_shape=(far, far, far), in_specs=[smem] + [anyw...]
    all_to_all x3, waiting for transfers between devices: 7.85 us -> 9.01 us  [exchange(): return lax.all_to_all(pieces, axis, split_axis=0, concat_axis=0, tiled=True)]
  transfers between devices with their start and end apart: 4 -> 4, of which waited for: 2 -> 3; matrix products, arithmetic and copies ran while one was open for 1% -> 1% of each run, Pallas kernels for 32% -> 32%
where the time goes in v3:
time: 85.2 us; the launch traced here: 84.7 us
  Pallas kernels  40.6 us (48%)
  starting transfers between devices  32.7 us (38%)
  waiting for transfers between devices  9.01 us (11%)
  local copies, waits for them, and re-layouts  1.44 us (2%)
  between operations  0.88 us (1%)
    all_to_all x3, starting transfers between devices, exchange(): return lax.all_to_all(pieces, axis, split_axis=0, concat_axis=0, tiled=True)  27.6 us
    pallas_call x1, Pallas kernels, prep_first(): pl.pallas_call(prep_a, out_shape=(mat,) * 4, name='prep_a')(dyn, prior)  11.3 us
    pallas_call x1, Pallas kernels, time_scans(): pl.pallas_call(scans, out_shape=(out, out), in_specs=[smem] + [anywhere]...  11.2 us
    all_to_all x3, waiting for transfers between devices, exchange(): return lax.all_to_all(pieces, axis, split_axis=0, concat_axis=0, tiled=True)  9.01 us
    pallas_call x1, Pallas kernels, prep_second(): pl.pallas_call(prep_b, out_shape=(mat, half, mat), scratch_shapes=[vm()],...  8.09 us
    pallas_call x1, Pallas kernels, inverse(): pl.pallas_call(invert, out_shape=(far, far, far), in_specs=[smem] + [anyw...  7.49 us
    ppermute x1, starting transfers between devices, shards(): other = lax.ppermute(own, 'tm', [(i, i ^ 1) for i in range(16)])  5.09 us
    pallas_call x1, Pallas kernels, local_partials(): pl.pallas_call(partials, out_shape=jax.ShapeDtypeStruct((32 * ROWS, 128),...  2.6 us
  transfers between devices with their start and end apart: 4, of which 3 were waited for; matrix products, arithmetic and copies ran while one was open for 1% of the time, Pallas kernels for 32%

profile of v3, /device:TPU:1, one launch (start us, length us, event | category | flops | bytes accessed | tf_op | source)
XLA Modules:
  0.0 84.7 jit_solution(5941486805068818945)
XLA Ops:
  0.6 2.6 %partials.1 = f32[768,128]{1,0:T(8,128)} custom-call(s32[1]{0:T(128)} %bitcast.tm_ref, f32[4,512]{1,0:T(4,128)} %obs_ref.1, bf16[512,512]{1,0:T(8,128)(2,1)} %load_ref.1, f32[1,512]{1,0:T(1,128)} %bitcast.10), custom_call_target="tpu_custom_call" | custom-call | tf_op jit(solution)/shard_map/partials/pallas_call | solution.py:381
  3.2 10.5 %all-to-all-start = ((f32[32,24,128]{2,1,0:T(8,128)}), f32[32,24,128]{2,1,0:T(8,128)S(1)}, u32[]{:S(2)}, u32[]{:S(2)}) async-start(f32[32,24,128]{2,1,0:T(8,128)} %bitcast.9), calls=%async_computation | async-start | bytes 786432 | tf_op jit(solution)/shard_map/all_to_all | solution.py:390
  13.7 11.3 %prep_a.1 = (f32[512,512]{1,0:T(8,128)}, f32[512,512]{1,0:T(8,128)}, f32[512,512]{1,0:T(8,128)}, f32[512,512]{1,0:T(8,128)}) custom-call(f32[512,512]{1,0:T(8,128)} %dyn_ref.1, f32[512,512]{1,0:T(8,128)} %refs_6_), custom_call_target="tpu_custom_call" | custom-call | tf_op jit(solution)/shard_map/prep_a/pallas_call | solution.py:347
  25.0 2.5 %all-to-all-done = f32[32,24,128]{2,1,0:T(8,128)S(1)} async-done(((f32[32,24,128]{2,1,0:T(8,128)}), f32[32,24,128]{2,1,0:T(8,128)S(1)}, u32[]{:S(2)}, u32[]{:S(2)}) %all-to-all-start) | async-done | bytes 393248 | tf_op jit(solution)/shard_map/all_to_all | solution.py:390
  27.6 0.8 broadcast_in_dim.6
  28.4 6.7 %all-to-all-start.1 = ((f32[32,24,128]{2,1,0:T(8,128)}), f32[32,24,128]{2,1,0:T(8,128)S(1)}, u32[]{:S(2)}, u32[]{:S(2)}) async-start(f32[32,24,128]{2,1,0:T(8,128)} %broadcast_in_dim.6), calls=%async_computation.1 | async-start | bytes 786432 | tf_op jit(solution)/shard_map/all_to_all | solution.py:390
  35.0 8.1 %prep_b.1 = (f32[512,512]{1,0:T(8,128)}, bf16[512,512]{1,0:T(8,128)(2,1)}, f32[512,512]{1,0:T(8,128)}) custom-call(f32[512,512]{1,0:T(8,128)} %refs_6_, f32[512,512]{1,0:T(8,128)} %dyn_ref.1, f32[512,512]{1,0:T(8,128)} %get-tuple-element.24.x_in), custom_call_target="tpu_custom_call" | custom-call | tf_op jit(solution)/shard_map/prep_b/pallas_call | solution.py:351
  43.1 5.1 %all-to-all-done.1 = f32[32,24,128]{2,1,0:T(8,128)S(1)} async-done(((f32[32,24,128]{2,1,0:T(8,128)}), f32[32,24,128]{2,1,0:T(8,128)S(1)}, u32[]{:S(2)}, u32[]{:S(2)}) %all-to-all-start.1) | async-done | bytes 393248 | tf_op jit(solution)/shard_map/all_to_all | solution.py:390
  48.2 5.1 %collective-permute-start = (f32[768,128]{1,0:T(8,128)S(1)}, f32[768,128]{1,0:T(8,128)S(1)}, u32[]{:S(2)}, u32[]{:S(2)}) collective-permute-start(f32[768,128]{1,0:T(8,128)S(1)} %bitcast.5), channel_id=1, source_target_pairs={{0,1},{1,0},{2,3},{3,2},{4,5},{5,4},{6,7},{7,6},{8,9},{9,8},{10,11... | collective-permute-start | bytes 1179656 | tf_op jit(solution)/shard_map/ppermute | solution.py:404
  53.3 0.7 broadcast_in_dim.7
  54.0 10.4 %all-to-all-start.2 = ((f32[16,16,128]{2,1,0:T(8,128)}), f32[16,16,128]{2,1,0:T(8,128)S(1)}, u32[]{:S(2)}, u32[]{:S(2)}) async-start(f32[16,16,128]{2,1,0:T(8,128)} %broadcast_in_dim.7), calls=%async_computation.2 | async-start | bytes 262144 | tf_op jit(solution)/shard_map/all_to_all | solution.py:390
  64.5 0.0 collective-permute-done.refs_1_
  64.5 7.5 %invert.1 = (f32[512,512]{1,0:T(8,128)}, f32[512,512]{1,0:T(8,128)}, f32[512,512]{1,0:T(8,128)}) custom-call(s32[1]{0:T(128)} %bitcast.tm_ref, f32[768,128]{1,0:T(8,128)S(1)} %bitcast.7, f32[768,128]{1,0:T(8,128)S(1)} %collective-permute-done.refs_1_, f32[512,512]{1,0:T(8,128)} %get-tuple-element.27.refs_2_, bf16[512,512]{1,0:T(8,128)(2,1)} %get-tuple-element.28.refs_3_, ...), custom_call_target="tpu_custom_call" | custom-call | tf_op jit(solution)/shard_map/invert/pallas_call | solution.py:356
  72.0 1.4 %all-to-all-done.2 = f32[16,16,128]{2,1,0:T(8,128)S(1)} async-done(((f32[16,16,128]{2,1,0:T(8,128)}), f32[16,16,128]{2,1,0:T(8,128)S(1)}, u32[]{:S(2)}, u32[]{:S(2)}) %all-to-all-start.2) | async-done | bytes 131104 | tf_op jit(solution)/shard_map/all_to_all | solution.py:390
  73.3 11.2 %scans.1 = (f32[4,512]{1,0:T(4,128)}, f32[4,512]{1,0:T(4,128)}) custom-call(s32[1]{0:T(128)} %bitcast.tm_ref, f32[512,512]{1,0:T(8,128)} %get-tuple-element.32.refs_0_, f32[256,128]{1,0:T(8,128)S(1)} %bitcast.8, f32[512,512]{1,0:T(8,128)} %get-tuple-element.33.refs_2_, f32[512,512]{1,0:T(8,128)} %get-tuple-element.34.refs_3_, ...), custom_call_target="tpu_custom_call" | custom-call | tf_op jit(solution)/shard_map/scans/pallas_call | solution.py:370
  (2 shorter events, 0.0 us)
Async XLA Ops:
  3.2 24.3 %all-to-all-start = ((f32[32,24,128]{2,1,0:T(8,128)}), f32[32,24,128]{2,1,0:T(8,128)S(1)}, u32[]{:S(2)}, u32[]{:S(2)}) async-start(f32[32,24,128]{2,1,0:T(8,128)} %bitcast.9), calls=%async_computation | async-start | bytes 786432 | tf_op jit(solution)/shard_map/all_to_all | solution.py:390
  28.4 19.9 %all-to-all-start.1 = ((f32[32,24,128]{2,1,0:T(8,128)}), f32[32,24,128]{2,1,0:T(8,128)S(1)}, u32[]{:S(2)}, u32[]{:S(2)}) async-start(f32[32,24,128]{2,1,0:T(8,128)} %broadcast_in_dim.6), calls=%async_computation.1 | async-start | bytes 786432 | tf_op jit(solution)/shard_map/all_to_all | solution.py:390
  48.2 16.2 %collective-permute-start = (f32[768,128]{1,0:T(8,128)S(1)}, f32[768,128]{1,0:T(8,128)S(1)}, u32[]{:S(2)}, u32[]{:S(2)}) collective-permute-start(f32[768,128]{1,0:T(8,128)S(1)} %bitcast.5), channel_id=1, source_target_pairs={{0,1},{1,0},{2,3},{3,2},{4,5},{5,4},{6,7},{7,6},{8,9},{9,8},{10,11... | collective-permute-start | bytes 1179656 | tf_op jit(solution)/shard_map/ppermute | solution.py:404
  54.0 19.3 %all-to-all-start.2 = ((f32[16,16,128]{2,1,0:T(8,128)}), f32[16,16,128]{2,1,0:T(8,128)S(1)}, u32[]{:S(2)}, u32[]{:S(2)}) async-start(f32[16,16,128]{2,1,0:T(8,128)} %broadcast_in_dim.7), calls=%async_computation.2 | async-start | bytes 262144 | tf_op jit(solution)/shard_map/all_to_all | solution.py:390

commit v4 on v3

--- a/solution.py
+++ b/solution.py
@@ -165,7 +165,7 @@
     return dot3(split(a), split(b))
 
 
-def prep_b(prior_ref, dyn_ref, x_in, x_ref, rest_ref, wp_ref, r_ref):
+def prep_b(prior_ref, dyn_ref, x_in, x_ref, rest_ref, wp_ref, c_ref, r_ref):
     x_ref[...] = x_in[...]
     n2 = refine(lambda v: fine(prior_ref[...], v), x_ref, r_ref, 1e-5, 40, coarse)
 
@@ -183,6 +183,8 @@
     rest_ref[...] = rest.astype(bf16)
     turned = dyn_ref[...].T
     wp_ref[...] = turned - coarse(turned, rest)
+    mean = jnp.sum(jnp.sum(turned * eye(), axis=0, keepdims=True), axis=1, keepdims=True) * (1.0 / R)
+    c_ref[...] = jnp.broadcast_to(mean, (8, 128))
 
 
 PAIRS = ((0, 0), (0, 1), (0, 2), (0, 3), (1, 1), (1, 2), (1, 3), (2, 2), (2, 3), (3, 3))
@@ -193,15 +195,14 @@
 
 
 def invert(tm_ref, *refs):
-    sources, results, held, made, (g_ref, r_ref, sems, out_sems) = refs[:8], refs[8:11], refs[11:19], refs[19:22], refs[22:]
-    own_ref, other_ref, pinv_ref, rest_ref, wp_ref, q_ref, prior_ref, wt_ref = held
+    sources, results, held, made, (g_ref, r_ref, sems, out_sems) = refs[2:8], refs[8:11], refs[11:17], refs[17:20], refs[20:]
+    own_ref, other_ref = refs[:2]
+    pinv_ref, rest_ref, wp_ref, q_ref, prior_ref, wt_ref = held
     x_ref, ft_ref, m_ref = made
     loads = copies(sources, held, sems)
     stores = copies(made, results, out_sems)
     for c in loads[:4]:
         c.start()
-    loads[0].wait()
-    loads[1].wait()
     first = lax.rem(tm_ref[0], 2) == 0
     for n, (i, j) in enumerate(PAIRS):
         at = (n % 5) * 128
@@ -211,10 +212,8 @@
         if i != j:
             g_ref[128 * j : 128 * j + 128, 128 * i : 128 * i + 128] = blk.T
     gram = g_ref[...]
-    loads[2].wait()
-    loads[3].wait()
-    loads[4].start()
-    loads[5].start()
+    loads[0].wait()
+    loads[1].wait()
     psplit = split(pinv_ref[...])
     h = dot3(split(gram), psplit) - rest_ref[...].astype(f32)
     h0, h1 = split(h)
@@ -225,8 +224,8 @@
     r = r + rr + dot1(rh, rr.astype(bf16))
     s = r - h0.astype(f32) - dot1(h0, r.astype(bf16))
     ss = split(s)
-    loads[4].wait()
-    loads[5].wait()
+    loads[2].wait()
+    loads[3].wait()
     m_ref[...] = gram + q_ref[...]
     stores[2].start()
     wp = wp_ref[...]
@@ -241,7 +240,7 @@
 
     @pl.when(jnp.logical_not(good))
     def _():
-        for c in loads[6:]:
+        for c in loads[4:]:
             c.start()
             c.wait()
         e = coarse(g_ref[...], pinv_ref[...])
@@ -263,18 +262,18 @@
 
 
 def scans(tm_ref, *refs):
-    sources, (filt_ref, smooth_ref), held, (f_ref, s_ref, sems) = refs[:5], refs[5:7], refs[7:12], refs[12:]
-    ft_ref, info_ref, x_ref, m_ref, nn_ref = held
+    sources, (filt_ref, smooth_ref), held, (f_ref, s_ref, sems) = refs[:6], refs[6:8], refs[8:14], refs[14:]
+    ft_ref, info_ref, x_ref, m_ref, nn_ref, c_ref = held
     loads = copies(sources, held, sems)
     for c in loads:
         c.start()
     T = 64
     loads[0].wait()
+    loads[5].wait()
     f = ft_ref[...]
     powers = [split(f)]
-    ident = eye()
-    c = jnp.sum(jnp.sum(f * ident, axis=0, keepdims=True), axis=1, keepdims=True) * (1.0 / R)
-    e = f - c * ident
+    c = c_ref[0:1, 0:1]
+    e = f - c * eye()
     es = split(e)
     f = c * (f + e) + dot3(es, es)
     powers.append(split(f))
@@ -328,6 +327,7 @@
 vm = partial(pltpu.VMEM, (R, R), f32)
 mat = jax.ShapeDtypeStruct((R, R), f32)
 half = jax.ShapeDtypeStruct((R, R), bf16)
+tile = jax.ShapeDtypeStruct((8, 128), f32)
 smem = pl.BlockSpec(memory_space=pltpu.SMEM)
 vmem = pl.BlockSpec(memory_space=pltpu.VMEM)
 room = pltpu.CompilerParams(vmem_limit_bytes=28 << 20)
@@ -337,6 +337,10 @@
 far = pltpu.HBM((R, R), f32)
 
 
+def near(arrays):
+    return [pltpu.with_memory_space_constraint(a, pltpu.VMEM) for a in arrays]
+
+
 def kept_far(arrays):
     return [pltpu.with_memory_space_constraint(a, pltpu.HBM) for a in arrays]
 
@@ -348,7 +352,7 @@
 
 
 def prep_second(prior, dyn, x):
-    return pl.pallas_call(prep_b, out_shape=(mat, half, mat), scratch_shapes=[vm()], name="prep_b")(prior, dyn, x)
+    return pl.pallas_call(prep_b, out_shape=(mat, half, mat, tile), scratch_shapes=[vm()], name="prep_b")(prior, dyn, x)
 
 
 def inverse(tm, *arrays):
@@ -356,12 +360,12 @@
     return pl.pallas_call(
         invert,
         out_shape=(far, far, far),
-        in_specs=[smem] + [anywhere] * 8,
+        in_specs=[smem] + [vmem] * 2 + [anywhere] * 6,
         out_specs=(anywhere,) * 3,
-        scratch_shapes=[part, part, vm(), pltpu.VMEM((R, R), bf16)] + [vm()] * 9 + [dma((8,)), dma((3,))],
+        scratch_shapes=[vm(), pltpu.VMEM((R, R), bf16)] + [vm()] * 9 + [dma((6,)), dma((3,))],
         name="invert",
         compiler_params=room,
-    )(tm, *arrays[:2], *kept_far(arrays[2:]))
+    )(tm, *near(arrays[:2]), *kept_far(arrays[2:]))
 
 
 def time_scans(tm, *arrays):
@@ -370,8 +374,8 @@
     return pl.pallas_call(
         scans,
         out_shape=(out, out),
-        in_specs=[smem] + [anywhere] * 5,
-        scratch_shapes=[vm(), pltpu.VMEM((256, 128), f32), vm(), vm(), vm(), rows, rows, pltpu.SemaphoreType.DMA((5,))],
+        in_specs=[smem] + [anywhere] * 6,
+        scratch_shapes=[vm(), pltpu.VMEM((256, 128), f32), vm(), vm(), vm(), pltpu.VMEM((8, 128), f32), rows, rows, pltpu.SemaphoreType.DMA((6,))],
         name="scans",
         compiler_params=room,
     )(tm, *kept_far(arrays[:1]), arrays[1], *kept_far(arrays[2:]))
@@ -399,13 +403,13 @@
     total = jnp.broadcast_to(pieces.sum(axis=0), pieces.shape)
     total, x0 = lax.optimization_barrier((total, x0))
     own = exchange(total, "sens").reshape(32 * ROWS, 128)
-    pinv, rest, wp = prep_second(prior_prec, dynamics, x0)
+    pinv, rest, wp, c = prep_second(prior_prec, dynamics, x0)
     own, pinv = lax.optimization_barrier((own, pinv))
     other = lax.ppermute(own, "tm", [(i, i ^ 1) for i in range(16)])
     info = jnp.broadcast_to(own[INFO : INFO + 16], (16, 16, 128))
     info = exchange(info, "tm").reshape(256, 128)
     x, ft, m = inverse(tm, own, other, pinv, rest, wp, q, prior_prec, wt)
-    return time_scans(tm, ft, info, x, m, nn)
+    return time_scans(tm, ft, info, x, m, nn, c)
 
 
 def solution(mesh):

time: 85.2 us -> 85.7 us (level)
  transfers between devices with their start and end apart: 4 -> 4, of which waited for: 3 -> 3; matrix products, arithmetic and copies ran while one was open for 1% -> 1% of each run, Pallas kernels for 32% -> 31%
where the time goes in v4:
time: 85.7 us; the launch traced here: 85.2 us
  Pallas kernels  40.8 us (48%)
  starting transfers between devices  32.7 us (38%)
  waiting for transfers between devices  9.4 us (11%)
  local copies, waits for them, and re-layouts  1.44 us (2%)
  between operations  0.88 us (1%)
    all_to_all x3, starting transfers between devices, exchange(): return lax.all_to_all(pieces, axis, split_axis=0, concat_axis=0, tiled=True)  27.6 us
    pallas_call x1, Pallas kernels, time_scans(): pl.pallas_call(scans, out_shape=(out, out), in_specs=[smem] + [anywhere]...  11.7 us
    pallas_call x1, Pallas kernels, prep_first(): pl.pallas_call(prep_a, out_shape=(mat,) * 4, name='prep_a')(dyn, prior)  11.3 us
    all_to_all x3, waiting for transfers between devices, exchange(): return lax.all_to_all(pieces, axis, split_axis=0, concat_axis=0, tiled=True)  9.4 us
    pallas_call x1, Pallas kernels, prep_second(): pl.pallas_call(prep_b, out_shape=(mat, half, mat, tile), scratch_shapes=[...  8.09 us
    pallas_call x1, Pallas kernels, inverse(): pl.pallas_call(invert, out_shape=(far, far, far), in_specs=[smem] + [vmem...  7.11 us
    ppermute x1, starting transfers between devices, shards(): other = lax.ppermute(own, 'tm', [(i, i ^ 1) for i in range(16)])  5.09 us
    pallas_call x1, Pallas kernels, local_partials(): pl.pallas_call(partials, out_shape=jax.ShapeDtypeStruct((32 * ROWS, 128),...  2.6 us
  transfers between devices with their start and end apart: 4, of which 3 were waited for; matrix products, arithmetic and copies ran while one was open for 1% of the time, Pallas kernels for 31%

profile of v4, /device:TPU:1, one launch (start us, length us, event | category | flops | bytes accessed | tf_op | source)
XLA Modules:
  0.0 85.2 jit_solution(10263144314486463290)
XLA Ops:
  0.6 2.6 %partials.1 = f32[768,128]{1,0:T(8,128)} custom-call(s32[1]{0:T(128)} %bitcast.tm_ref, f32[4,512]{1,0:T(4,128)} %obs_ref.1, bf16[512,512]{1,0:T(8,128)(2,1)} %load_ref.1, f32[1,512]{1,0:T(1,128)} %bitcast.10), custom_call_target="tpu_custom_call" | custom-call | tf_op jit(solution)/shard_map/partials/pallas_call | solution.py:385
  3.2 10.5 %all-to-all-start = ((f32[32,24,128]{2,1,0:T(8,128)}), f32[32,24,128]{2,1,0:T(8,128)S(1)}, u32[]{:S(2)}, u32[]{:S(2)}) async-start(f32[32,24,128]{2,1,0:T(8,128)} %bitcast.9), calls=%async_computation | async-start | bytes 786432 | tf_op jit(solution)/shard_map/all_to_all | solution.py:394
  13.7 11.3 %prep_a.1 = (f32[512,512]{1,0:T(8,128)}, f32[512,512]{1,0:T(8,128)}, f32[512,512]{1,0:T(8,128)}, f32[512,512]{1,0:T(8,128)}) custom-call(f32[512,512]{1,0:T(8,128)} %dyn_ref.1, f32[512,512]{1,0:T(8,128)} %refs_6_), custom_call_target="tpu_custom_call" | custom-call | tf_op jit(solution)/shard_map/prep_a/pallas_call | solution.py:351
  25.0 2.5 %all-to-all-done = f32[32,24,128]{2,1,0:T(8,128)S(1)} async-done(((f32[32,24,128]{2,1,0:T(8,128)}), f32[32,24,128]{2,1,0:T(8,128)S(1)}, u32[]{:S(2)}, u32[]{:S(2)}) %all-to-all-start) | async-done | bytes 393248 | tf_op jit(solution)/shard_map/all_to_all | solution.py:394
  27.6 0.8 broadcast_in_dim.6
  28.4 6.7 %all-to-all-start.1 = ((f32[32,24,128]{2,1,0:T(8,128)}), f32[32,24,128]{2,1,0:T(8,128)S(1)}, u32[]{:S(2)}, u32[]{:S(2)}) async-start(f32[32,24,128]{2,1,0:T(8,128)} %broadcast_in_dim.6), calls=%async_computation.1 | async-start | bytes 786432 | tf_op jit(solution)/shard_map/all_to_all | solution.py:394
  35.0 8.1 %prep_b.1 = (f32[512,512]{1,0:T(8,128)}, bf16[512,512]{1,0:T(8,128)(2,1)}, f32[512,512]{1,0:T(8,128)}, f32[8,128]{1,0:T(8,128)}) custom-call(f32[512,512]{1,0:T(8,128)} %refs_6_, f32[512,512]{1,0:T(8,128)} %dyn_ref.1, f32[512,512]{1,0:T(8,128)} %get-tuple-element.25.x_in), custom_call_target="tpu_custom_call" | custom-call | tf_op jit(solution)/shard_map/prep_b/pallas_call | solution.py:355
  43.1 5.1 %all-to-all-done.1 = f32[32,24,128]{2,1,0:T(8,128)S(1)} async-done(((f32[32,24,128]{2,1,0:T(8,128)}), f32[32,24,128]{2,1,0:T(8,128)S(1)}, u32[]{:S(2)}, u32[]{:S(2)}) %all-to-all-start.1) | async-done | bytes 393248 | tf_op jit(solution)/shard_map/all_to_all | solution.py:394
  48.2 5.1 %collective-permute-start = (f32[768,128]{1,0:T(8,128)S(1)}, f32[768,128]{1,0:T(8,128)S(1)}, u32[]{:S(2)}, u32[]{:S(2)}) collective-permute-start(f32[768,128]{1,0:T(8,128)S(1)} %bitcast.5), channel_id=1, source_target_pairs={{0,1},{1,0},{2,3},{3,2},{4,5},{5,4},{6,7},{7,6},{8,9},{9,8},{10,11... | collective-permute-start | bytes 1179656 | tf_op jit(solution)/shard_map/ppermute | solution.py:408
  53.3 0.7 broadcast_in_dim.7
  54.0 10.4 %all-to-all-start.2 = ((f32[16,16,128]{2,1,0:T(8,128)}), f32[16,16,128]{2,1,0:T(8,128)S(1)}, u32[]{:S(2)}, u32[]{:S(2)}) async-start(f32[16,16,128]{2,1,0:T(8,128)} %broadcast_in_dim.7), calls=%async_computation.2 | async-start | bytes 262144 | tf_op jit(solution)/shard_map/all_to_all | solution.py:394
  64.5 0.0 collective-permute-done.refs_1_
  64.5 7.1 %invert.1 = (f32[512,512]{1,0:T(8,128)}, f32[512,512]{1,0:T(8,128)}, f32[512,512]{1,0:T(8,128)}) custom-call(s32[1]{0:T(128)} %bitcast.tm_ref, f32[768,128]{1,0:T(8,128)S(1)} %bitcast.7, f32[768,128]{1,0:T(8,128)S(1)} %collective-permute-done.refs_1_, f32[512,512]{1,0:T(8,128)} %get-tuple-element.28.refs_2_, bf16[512,512]{1,0:T(8,128)(2,1)} %get-tuple-element.29.refs_3_, ...), custom_call_target="tpu_custom_call" | custom-call | tf_op jit(solution)/shard_map/invert/pallas_call | solution.py:360
  71.6 1.8 %all-to-all-done.2 = f32[16,16,128]{2,1,0:T(8,128)S(1)} async-done(((f32[16,16,128]{2,1,0:T(8,128)}), f32[16,16,128]{2,1,0:T(8,128)S(1)}, u32[]{:S(2)}, u32[]{:S(2)}) %all-to-all-start.2) | async-done | bytes 131104 | tf_op jit(solution)/shard_map/all_to_all | solution.py:394
  73.3 11.7 %scans.1 = (f32[4,512]{1,0:T(4,128)}, f32[4,512]{1,0:T(4,128)}) custom-call(s32[1]{0:T(128)} %bitcast.tm_ref, f32[512,512]{1,0:T(8,128)} %get-tuple-element.33.refs_0_, f32[256,128]{1,0:T(8,128)S(1)} %bitcast.8, f32[512,512]{1,0:T(8,128)} %get-tuple-element.34.refs_2_, f32[512,512]{1,0:T(8,128)} %get-tuple-element.35.refs_3_, ...), custom_call_target="tpu_custom_call" | custom-call | tf_op jit(solution)/shard_map/scans/pallas_call | solution.py:374
  (2 shorter events, 0.0 us)
Async XLA Ops:
  3.2 24.3 %all-to-all-start = ((f32[32,24,128]{2,1,0:T(8,128)}), f32[32,24,128]{2,1,0:T(8,128)S(1)}, u32[]{:S(2)}, u32[]{:S(2)}) async-start(f32[32,24,128]{2,1,0:T(8,128)} %bitcast.9), calls=%async_computation | async-start | bytes 786432 | tf_op jit(solution)/shard_map/all_to_all | solution.py:394
  28.4 19.9 %all-to-all-start.1 = ((f32[32,24,128]{2,1,0:T(8,128)}), f32[32,24,128]{2,1,0:T(8,128)S(1)}, u32[]{:S(2)}, u32[]{:S(2)}) async-start(f32[32,24,128]{2,1,0:T(8,128)} %broadcast_in_dim.6), calls=%async_computation.1 | async-start | bytes 786432 | tf_op jit(solution)/shard_map/all_to_all | solution.py:394
  48.2 16.2 %collective-permute-start = (f32[768,128]{1,0:T(8,128)S(1)}, f32[768,128]{1,0:T(8,128)S(1)}, u32[]{:S(2)}, u32[]{:S(2)}) collective-permute-start(f32[768,128]{1,0:T(8,128)S(1)} %bitcast.5), channel_id=1, source_target_pairs={{0,1},{1,0},{2,3},{3,2},{4,5},{5,4},{6,7},{7,6},{8,9},{9,8},{10,11... | collective-permute-start | bytes 1179656 | tf_op jit(solution)/shard_map/ppermute | solution.py:408
  54.0 19.3 %all-to-all-start.2 = ((f32[16,16,128]{2,1,0:T(8,128)}), f32[16,16,128]{2,1,0:T(8,128)S(1)}, u32[]{:S(2)}, u32[]{:S(2)}) async-start(f32[16,16,128]{2,1,0:T(8,128)} %broadcast_in_dim.7), calls=%async_computation.2 | async-start | bytes 262144 | tf_op jit(solution)/shard_map/all_to_all | solution.py:394

commit v5 on v4

--- a/solution.py
+++ b/solution.py
@@ -265,7 +265,7 @@
     sources, (filt_ref, smooth_ref), held, (f_ref, s_ref, sems) = refs[:6], refs[6:8], refs[8:14], refs[14:]
     ft_ref, info_ref, x_ref, m_ref, nn_ref, c_ref = held
     loads = copies(sources, held, sems)
-    for c in loads:
+    for c in loads[5:] + loads[:5]:
         c.start()
     T = 64
     loads[0].wait()

time: 85.7 us -> 84.9 us (level)
  no operation moved by 1% of the time
where the time goes in v5:
time: 84.9 us; the launch traced here: 84.4 us
  Pallas kernels  40 us (47%)
  starting transfers between devices  32.7 us (39%)
  waiting for transfers between devices  9.4 us (11%)
  local copies, waits for them, and re-layouts  1.44 us (2%)
  between operations  0.88 us (1%)
    all_to_all x3, starting transfers between devices, exchange(): return lax.all_to_all(pieces, axis, split_axis=0, concat_axis=0, tiled=True)  27.6 us
    pallas_call x1, Pallas kernels, prep_first(): pl.pallas_call(prep_a, out_shape=(mat,) * 4, name='prep_a')(dyn, prior)  11.3 us
    pallas_call x1, Pallas kernels, time_scans(): pl.pallas_call(scans, out_shape=(out, out), in_specs=[smem] + [anywhere]...  10.9 us
    all_to_all x3, waiting for transfers between devices, exchange(): return lax.all_to_all(pieces, axis, split_axis=0, concat_axis=0, tiled=True)  9.4 us
    pallas_call x1, Pallas kernels, prep_second(): pl.pallas_call(prep_b, out_shape=(mat, half, mat, tile), scratch_shapes=[...  8.09 us
    pallas_call x1, Pallas kernels, inverse(): pl.pallas_call(invert, out_shape=(far, far, far), in_specs=[smem] + [vmem...  7.11 us
    ppermute x1, starting transfers between devices, shards(): other = lax.ppermute(own, 'tm', [(i, i ^ 1) for i in range(16)])  5.09 us
    pallas_call x1, Pallas kernels, local_partials(): pl.pallas_call(partials, out_shape=jax.ShapeDtypeStruct((32 * ROWS, 128),...  2.6 us
  transfers between devices with their start and end apart: 4, of which 3 were waited for; matrix products, arithmetic and copies ran while one was open for 1% of the time, Pallas kernels for 31%

profile of v5, /device:TPU:1, one launch (start us, length us, event | category | flops | bytes accessed | tf_op | source)
XLA Modules:
  0.0 84.4 jit_solution(12663669565301911551)
XLA Ops:
  0.6 2.6 %partials.1 = f32[768,128]{1,0:T(8,128)} custom-call(s32[1]{0:T(128)} %bitcast.tm_ref, f32[4,512]{1,0:T(4,128)} %obs_ref.1, bf16[512,512]{1,0:T(8,128)(2,1)} %load_ref.1, f32[1,512]{1,0:T(1,128)} %bitcast.10), custom_call_target="tpu_custom_call" | custom-call | tf_op jit(solution)/shard_map/partials/pallas_call | solution.py:385
  3.2 10.5 %all-to-all-start = ((f32[32,24,128]{2,1,0:T(8,128)}), f32[32,24,128]{2,1,0:T(8,128)S(1)}, u32[]{:S(2)}, u32[]{:S(2)}) async-start(f32[32,24,128]{2,1,0:T(8,128)} %bitcast.9), calls=%async_computation | async-start | bytes 786432 | tf_op jit(solution)/shard_map/all_to_all | solution.py:394
  13.7 11.3 %prep_a.1 = (f32[512,512]{1,0:T(8,128)}, f32[512,512]{1,0:T(8,128)}, f32[512,512]{1,0:T(8,128)}, f32[512,512]{1,0:T(8,128)}) custom-call(f32[512,512]{1,0:T(8,128)} %dyn_ref.1, f32[512,512]{1,0:T(8,128)} %refs_6_), custom_call_target="tpu_custom_call" | custom-call | tf_op jit(solution)/shard_map/prep_a/pallas_call | solution.py:351
  25.0 2.5 %all-to-all-done = f32[32,24,128]{2,1,0:T(8,128)S(1)} async-done(((f32[32,24,128]{2,1,0:T(8,128)}), f32[32,24,128]{2,1,0:T(8,128)S(1)}, u32[]{:S(2)}, u32[]{:S(2)}) %all-to-all-start) | async-done | bytes 393248 | tf_op jit(solution)/shard_map/all_to_all | solution.py:394
  27.6 0.8 broadcast_in_dim.6
  28.4 6.7 %all-to-all-start.1 = ((f32[32,24,128]{2,1,0:T(8,128)}), f32[32,24,128]{2,1,0:T(8,128)S(1)}, u32[]{:S(2)}, u32[]{:S(2)}) async-start(f32[32,24,128]{2,1,0:T(8,128)} %broadcast_in_dim.6), calls=%async_computation.1 | async-start | bytes 786432 | tf_op jit(solution)/shard_map/all_to_all | solution.py:394
  35.0 8.1 %prep_b.1 = (f32[512,512]{1,0:T(8,128)}, bf16[512,512]{1,0:T(8,128)(2,1)}, f32[512,512]{1,0:T(8,128)}, f32[8,128]{1,0:T(8,128)}) custom-call(f32[512,512]{1,0:T(8,128)} %refs_6_, f32[512,512]{1,0:T(8,128)} %dyn_ref.1, f32[512,512]{1,0:T(8,128)} %get-tuple-element.25.x_in), custom_call_target="tpu_custom_call" | custom-call | tf_op jit(solution)/shard_map/prep_b/pallas_call | solution.py:355
  43.1 5.1 %all-to-all-done.1 = f32[32,24,128]{2,1,0:T(8,128)S(1)} async-done(((f32[32,24,128]{2,1,0:T(8,128)}), f32[32,24,128]{2,1,0:T(8,128)S(1)}, u32[]{:S(2)}, u32[]{:S(2)}) %all-to-all-start.1) | async-done | bytes 393248 | tf_op jit(solution)/shard_map/all_to_all | solution.py:394
  48.2 5.1 %collective-permute-start = (f32[768,128]{1,0:T(8,128)S(1)}, f32[768,128]{1,0:T(8,128)S(1)}, u32[]{:S(2)}, u32[]{:S(2)}) collective-permute-start(f32[768,128]{1,0:T(8,128)S(1)} %bitcast.5), channel_id=1, source_target_pairs={{0,1},{1,0},{2,3},{3,2},{4,5},{5,4},{6,7},{7,6},{8,9},{9,8},{10,11... | collective-permute-start | bytes 1179656 | tf_op jit(solution)/shard_map/ppermute | solution.py:408
  53.3 0.7 broadcast_in_dim.7
  54.0 10.4 %all-to-all-start.2 = ((f32[16,16,128]{2,1,0:T(8,128)}), f32[16,16,128]{2,1,0:T(8,128)S(1)}, u32[]{:S(2)}, u32[]{:S(2)}) async-start(f32[16,16,128]{2,1,0:T(8,128)} %broadcast_in_dim.7), calls=%async_computation.2 | async-start | bytes 262144 | tf_op jit(solution)/shard_map/all_to_all | solution.py:394
  64.5 0.0 collective-permute-done.refs_1_
  64.5 7.1 %invert.1 = (f32[512,512]{1,0:T(8,128)}, f32[512,512]{1,0:T(8,128)}, f32[512,512]{1,0:T(8,128)}) custom-call(s32[1]{0:T(128)} %bitcast.tm_ref, f32[768,128]{1,0:T(8,128)S(1)} %bitcast.7, f32[768,128]{1,0:T(8,128)S(1)} %collective-permute-done.refs_1_, f32[512,512]{1,0:T(8,128)} %get-tuple-element.28.refs_2_, bf16[512,512]{1,0:T(8,128)(2,1)} %get-tuple-element.29.refs_3_, ...), custom_call_target="tpu_custom_call" | custom-call | tf_op jit(solution)/shard_map/invert/pallas_call | solution.py:360
  71.6 1.8 %all-to-all-done.2 = f32[16,16,128]{2,1,0:T(8,128)S(1)} async-done(((f32[16,16,128]{2,1,0:T(8,128)}), f32[16,16,128]{2,1,0:T(8,128)S(1)}, u32[]{:S(2)}, u32[]{:S(2)}) %all-to-all-start.2) | async-done | bytes 131104 | tf_op jit(solution)/shard_map/all_to_all | solution.py:394
  73.3 10.9 %scans.1 = (f32[4,512]{1,0:T(4,128)}, f32[4,512]{1,0:T(4,128)}) custom-call(s32[1]{0:T(128)} %bitcast.tm_ref, f32[512,512]{1,0:T(8,128)} %get-tuple-element.33.refs_0_, f32[256,128]{1,0:T(8,128)S(1)} %bitcast.8, f32[512,512]{1,0:T(8,128)} %get-tuple-element.34.refs_2_, f32[512,512]{1,0:T(8,128)} %get-tuple-element.35.refs_3_, ...), custom_call_target="tpu_custom_call" | custom-call | tf_op jit(solution)/shard_map/scans/pallas_call | solution.py:374
  (2 shorter events, 0.0 us)
Async XLA Ops:
  3.2 24.3 %all-to-all-start = ((f32[32,24,128]{2,1,0:T(8,128)}), f32[32,24,128]{2,1,0:T(8,128)S(1)}, u32[]{:S(2)}, u32[]{:S(2)}) async-start(f32[32,24,128]{2,1,0:T(8,128)} %bitcast.9), calls=%async_computation | async-start | bytes 786432 | tf_op jit(solution)/shard_map/all_to_all | solution.py:394
  28.4 19.9 %all-to-all-start.1 = ((f32[32,24,128]{2,1,0:T(8,128)}), f32[32,24,128]{2,1,0:T(8,128)S(1)}, u32[]{:S(2)}, u32[]{:S(2)}) async-start(f32[32,24,128]{2,1,0:T(8,128)} %broadcast_in_dim.6), calls=%async_computation.1 | async-start | bytes 786432 | tf_op jit(solution)/shard_map/all_to_all | solution.py:394
  48.2 16.2 %collective-permute-start = (f32[768,128]{1,0:T(8,128)S(1)}, f32[768,128]{1,0:T(8,128)S(1)}, u32[]{:S(2)}, u32[]{:S(2)}) collective-permute-start(f32[768,128]{1,0:T(8,128)S(1)} %bitcast.5), channel_id=1, source_target_pairs={{0,1},{1,0},{2,3},{3,2},{4,5},{5,4},{6,7},{7,6},{8,9},{9,8},{10,11... | collective-permute-start | bytes 1179656 | tf_op jit(solution)/shard_map/ppermute | solution.py:408
  54.0 19.3 %all-to-all-start.2 = ((f32[16,16,128]{2,1,0:T(8,128)}), f32[16,16,128]{2,1,0:T(8,128)S(1)}, u32[]{:S(2)}, u32[]{:S(2)}) async-start(f32[16,16,128]{2,1,0:T(8,128)} %broadcast_in_dim.7), calls=%async_computation.2 | async-start | bytes 262144 | tf_op jit(solution)/shard_map/all_to_all | solution.py:394

commit v6 on v5

--- a/solution.py
+++ b/solution.py
@@ -378,7 +378,7 @@
         scratch_shapes=[vm(), pltpu.VMEM((256, 128), f32), vm(), vm(), vm(), pltpu.VMEM((8, 128), f32), rows, rows, pltpu.SemaphoreType.DMA((6,))],
         name="scans",
         compiler_params=room,
-    )(tm, *kept_far(arrays[:1]), arrays[1], *kept_far(arrays[2:]))
+    )(tm, *kept_far(arrays[:1]), arrays[1], *kept_far(arrays[2:5]), arrays[5])
 
 
 def local_partials(tm, observed, loadings, noise):

time: 84.9 us -> 85.6 us (level)
  no operation moved by 1% of the time
where the time goes in v6:
time: 85.6 us; the launch traced here: 85.1 us
  Pallas kernels  40 us (47%)
  starting transfers between devices  32.7 us (38%)
  waiting for transfers between devices  9.42 us (11%)
  local copies, waits for them, and re-layouts  2.11 us (2%)
  between operations  0.89 us (1%)
    all_to_all x3, starting transfers between devices, exchange(): return lax.all_to_all(pieces, axis, split_axis=0, concat_axis=0, tiled=True)  27.6 us
    pallas_call x1, Pallas kernels, prep_first(): pl.pallas_call(prep_a, out_shape=(mat,) * 4, name='prep_a')(dyn, prior)  11.3 us
    pallas_call x1, Pallas kernels, time_scans(): pl.pallas_call(scans, out_shape=(out, out), in_specs=[smem] + [anywhere]...  10.9 us
    all_to_all x3, waiting for transfers between devices, exchange(): return lax.all_to_all(pieces, axis, split_axis=0, concat_axis=0, tiled=True)  9.42 us
    pallas_call x1, Pallas kernels, prep_second(): pl.pallas_call(prep_b, out_shape=(mat, half, mat, tile), scratch_shapes=[...  8.09 us
    pallas_call x1, Pallas kernels, inverse(): pl.pallas_call(invert, out_shape=(far, far, far), in_specs=[smem] + [vmem...  7.1 us
    ppermute x1, starting transfers between devices, shards(): other = lax.ppermute(own, 'tm', [(i, i ^ 1) for i in range(16)])  5.09 us
    pallas_call x1, Pallas kernels, local_partials(): pl.pallas_call(partials, out_shape=jax.ShapeDtypeStruct((32 * ROWS, 128),...  2.6 us
  transfers between devices with their start and end apart: 4, of which 3 were waited for; matrix products, arithmetic and copies ran while one was open for 1% of the time, Pallas kernels for 31%

profile of v6, /device:TPU:1, one launch (start us, length us, event | category | flops | bytes accessed | tf_op | source)
XLA Modules:
  0.0 85.1 jit_solution(7987088942065017972)
XLA Ops:
  0.6 2.6 %partials.1 = f32[768,128]{1,0:T(8,128)} custom-call(s32[1]{0:T(128)} %bitcast.tm_ref, f32[4,512]{1,0:T(4,128)} %obs_ref.1, bf16[512,512]{1,0:T(8,128)(2,1)} %load_ref.1, f32[1,512]{1,0:T(1,128)} %bitcast.10), custom_call_target="tpu_custom_call" | custom-call | tf_op jit(solution)/shard_map/partials/pallas_call | solution.py:385
  3.2 10.5 %all-to-all-start = ((f32[32,24,128]{2,1,0:T(8,128)}), f32[32,24,128]{2,1,0:T(8,128)S(1)}, u32[]{:S(2)}, u32[]{:S(2)}) async-start(f32[32,24,128]{2,1,0:T(8,128)} %bitcast.9), calls=%async_computation | async-start | bytes 786432 | tf_op jit(solution)/shard_map/all_to_all | solution.py:394
  13.7 11.3 %prep_a.1 = (f32[512,512]{1,0:T(8,128)}, f32[512,512]{1,0:T(8,128)}, f32[512,512]{1,0:T(8,128)}, f32[512,512]{1,0:T(8,128)}) custom-call(f32[512,512]{1,0:T(8,128)} %dyn_ref.1, f32[512,512]{1,0:T(8,128)} %refs_6_), custom_call_target="tpu_custom_call" | custom-call | tf_op jit(solution)/shard_map/prep_a/pallas_call | solution.py:351
  25.0 2.5 %all-to-all-done = f32[32,24,128]{2,1,0:T(8,128)S(1)} async-done(((f32[32,24,128]{2,1,0:T(8,128)}), f32[32,24,128]{2,1,0:T(8,128)S(1)}, u32[]{:S(2)}, u32[]{:S(2)}) %all-to-all-start) | async-done | bytes 393248 | tf_op jit(solution)/shard_map/all_to_all | solution.py:394
  27.6 0.8 broadcast_in_dim.6
  28.4 6.7 %all-to-all-start.1 = ((f32[32,24,128]{2,1,0:T(8,128)}), f32[32,24,128]{2,1,0:T(8,128)S(1)}, u32[]{:S(2)}, u32[]{:S(2)}) async-start(f32[32,24,128]{2,1,0:T(8,128)} %broadcast_in_dim.6), calls=%async_computation.1 | async-start | bytes 786432 | tf_op jit(solution)/shard_map/all_to_all | solution.py:394
  35.0 8.1 %prep_b.1 = (f32[512,512]{1,0:T(8,128)}, bf16[512,512]{1,0:T(8,128)(2,1)}, f32[512,512]{1,0:T(8,128)}, f32[8,128]{1,0:T(8,128)}) custom-call(f32[512,512]{1,0:T(8,128)} %refs_6_, f32[512,512]{1,0:T(8,128)} %dyn_ref.1, f32[512,512]{1,0:T(8,128)} %get-tuple-element.25.x_in), custom_call_target="tpu_custom_call" | custom-call | tf_op jit(solution)/shard_map/prep_b/pallas_call | solution.py:355
  43.1 5.1 %all-to-all-done.1 = f32[32,24,128]{2,1,0:T(8,128)S(1)} async-done(((f32[32,24,128]{2,1,0:T(8,128)}), f32[32,24,128]{2,1,0:T(8,128)S(1)}, u32[]{:S(2)}, u32[]{:S(2)}) %all-to-all-start.1) | async-done | bytes 393248 | tf_op jit(solution)/shard_map/all_to_all | solution.py:394
  48.2 5.1 %collective-permute-start = (f32[768,128]{1,0:T(8,128)S(1)}, f32[768,128]{1,0:T(8,128)S(1)}, u32[]{:S(2)}, u32[]{:S(2)}) collective-permute-start(f32[768,128]{1,0:T(8,128)S(1)} %bitcast.5), channel_id=1, source_target_pairs={{0,1},{1,0},{2,3},{3,2},{4,5},{5,4},{6,7},{7,6},{8,9},{9,8},{10,11... | collective-permute-start | bytes 1179656 | tf_op jit(solution)/shard_map/ppermute | solution.py:408
  53.3 0.7 broadcast_in_dim.7
  54.0 10.5 %all-to-all-start.2 = ((f32[16,16,128]{2,1,0:T(8,128)}), f32[16,16,128]{2,1,0:T(8,128)S(1)}, u32[]{:S(2)}, u32[]{:S(2)}) async-start(f32[16,16,128]{2,1,0:T(8,128)} %broadcast_in_dim.7), calls=%async_computation.2 | async-start | bytes 262144 | tf_op jit(solution)/shard_map/all_to_all | solution.py:394
  64.4 0.0 collective-permute-done.refs_1_
  64.5 7.1 %invert.1 = (f32[512,512]{1,0:T(8,128)}, f32[512,512]{1,0:T(8,128)}, f32[512,512]{1,0:T(8,128)}) custom-call(s32[1]{0:T(128)} %bitcast.tm_ref, f32[768,128]{1,0:T(8,128)S(1)} %bitcast.7, f32[768,128]{1,0:T(8,128)S(1)} %collective-permute-done.refs_1_, f32[512,512]{1,0:T(8,128)} %get-tuple-element.28.refs_2_, bf16[512,512]{1,0:T(8,128)(2,1)} %get-tuple-element.29.refs_3_, ...), custom_call_target="tpu_custom_call" | custom-call | tf_op jit(solution)/shard_map/invert/pallas_call | solution.py:360
  71.6 1.8 %all-to-all-done.2 = f32[16,16,128]{2,1,0:T(8,128)S(1)} async-done(((f32[16,16,128]{2,1,0:T(8,128)}), f32[16,16,128]{2,1,0:T(8,128)S(1)}, u32[]{:S(2)}, u32[]{:S(2)}) %all-to-all-start.2) | async-done | bytes 131104 | tf_op jit(solution)/shard_map/all_to_all | solution.py:394
  73.3 0.0 copy-start
  73.3 0.7 copy-done
  74.0 10.9 %scans.1 = (f32[4,512]{1,0:T(4,128)}, f32[4,512]{1,0:T(4,128)}) custom-call(s32[1]{0:T(128)} %bitcast.tm_ref, f32[512,512]{1,0:T(8,128)} %get-tuple-element.33.refs_0_, f32[256,128]{1,0:T(8,128)S(1)} %bitcast.8, f32[512,512]{1,0:T(8,128)} %get-tuple-element.34.refs_2_, f32[512,512]{1,0:T(8,128)} %get-tuple-element.35.refs_3_, ...), custom_call_target="tpu_custom_call" | custom-call | tf_op jit(solution)/shard_map/scans/pallas_call | solution.py:374
  (2 shorter events, 0.0 us)
Async XLA Ops:
  3.2 24.3 %all-to-all-start = ((f32[32,24,128]{2,1,0:T(8,128)}), f32[32,24,128]{2,1,0:T(8,128)S(1)}, u32[]{:S(2)}, u32[]{:S(2)}) async-start(f32[32,24,128]{2,1,0:T(8,128)} %bitcast.9), calls=%async_computation | async-start | bytes 786432 | tf_op jit(solution)/shard_map/all_to_all | solution.py:394
  28.4 19.9 %all-to-all-start.1 = ((f32[32,24,128]{2,1,0:T(8,128)}), f32[32,24,128]{2,1,0:T(8,128)S(1)}, u32[]{:S(2)}, u32[]{:S(2)}) async-start(f32[32,24,128]{2,1,0:T(8,128)} %broadcast_in_dim.6), calls=%async_computation.1 | async-start | bytes 786432 | tf_op jit(solution)/shard_map/all_to_all | solution.py:394
  48.2 16.2 %collective-permute-start = (f32[768,128]{1,0:T(8,128)S(1)}, f32[768,128]{1,0:T(8,128)S(1)}, u32[]{:S(2)}, u32[]{:S(2)}) collective-permute-start(f32[768,128]{1,0:T(8,128)S(1)} %bitcast.5), channel_id=1, source_target_pairs={{0,1},{1,0},{2,3},{3,2},{4,5},{5,4},{6,7},{7,6},{8,9},{9,8},{10,11... | collective-permute-start | bytes 1179656 | tf_op jit(solution)/shard_map/ppermute | solution.py:408
  54.0 19.3 %all-to-all-start.2 = ((f32[16,16,128]{2,1,0:T(8,128)}), f32[16,16,128]{2,1,0:T(8,128)S(1)}, u32[]{:S(2)}, u32[]{:S(2)}) async-start(f32[16,16,128]{2,1,0:T(8,128)} %broadcast_in_dim.7), calls=%async_computation.2 | async-start | bytes 262144 | tf_op jit(solution)/shard_map/all_to_all | solution.py:394
  73.3 0.7 copy-start
